TPU v7x, 1024 devices: a whole 4x8x16 slice. The times are simulated.
1024 devices in a mesh: seq: 32 (over z, core), exp: 4 (over x), ch: 8 (over y).
Axes of the slice: x: 4, y: 8, z: 16, core: 2. Of those that a mesh axis runs over, the one named last changes fastest.
Arguments:
- conv_x: bfloat16 [4096, 8192], P('seq', ('exp', 'ch')), may hold values from -6 to 6
- gate_z: bfloat16 [4096, 8192], P('seq', ('exp', 'ch')), may hold values from -6 to 6
- step: bfloat16 [4096, 8192], P('seq', ('exp', 'ch')), may hold values from 0 to 40962
- decay_rate: float32 [8192], P(('exp', 'ch')), may hold values from 0 to 1
- state_in: float32 [4096, 16], P('seq'), may hold values from -6 to 6
- state_out: float32 [4096, 16], P('seq'), may hold values from -6 to 6
- skip: float32 [8192], P(('exp', 'ch')), may hold values from 0.5 to 1.5
- out_weight: bfloat16 [8192, 4096], P(('exp', 'ch')), may hold values from -0.125 to 0.125
- residual: bfloat16 [4096, 4096], P('seq'), may hold values from -6 to 6
- norm_gain: float32 [4096], replicated, may hold values from 0.25 to 1.75
- expert_ids: int32 [4096, 2], P('seq'), may hold values from 0 to 15, all different within a row; in each aligned block of 128 rows (0 to 127, 128 to 255, ...) at most 18 rows name the same one
- expert_weights: bfloat16 [32, 1, 4096, 8, 1536], P('seq', None, 'exp', 'ch'), may hold values from -0.09375 to 0.09375
Outputs:
- expert_hidden: bfloat16 [32, 576, 1, 6144], P('seq', 'exp', None, 'ch')
Inputs may be any that keep to these rules, and one draw needn't show every extreme that they name: `expert_ids`: each token names 2 different experts. In each block of 128 tokens (the tokens of one index of seq) no expert is named more than 18 times, a bound that some block reaches.
All inputs are finite; a program needn't handle non-finite values.
Results may differ from a plain program's by a relative error of at most 0.03.
Values may be sent and summed in bfloat16 or wider, within the bound.
A program may use at most 32 MiB of HBM per device.

v0:
```python
import jax
import jax.numpy as jnp
from jax import lax
from jax.sharding import Mesh
from jax.sharding import PartitionSpec as P

D = 4096
EXPERTS = 16
TOP = 2
BLOCK = 32
SEQ = ("seq_0", "seq_1")


exact_products = lax.Precision.HIGHEST
norm_epsilon = 1e-05


def copy_for_each(array, axis):
    devices = lax.axis_size(axis)
    return lax.all_to_all(
        jnp.broadcast_to(array[None], (devices, *array.shape)), axis, 0, 0, tiled=True
    )


def gathered_once(array, axis):
    leaves = jax.tree.leaves(array)
    order = sorted(range(len(leaves)), key=lambda k: -leaves[k].size)
    width = (1, *leaves[order[0]].shape)[-1]
    lines = [
        jnp.pad(leaves[k].reshape(-1), (0, -leaves[k].size % width)).reshape(-1, width)
        for k in order
    ]
    both, at, found = (copy_for_each(jnp.concatenate(lines), axis), 0, {})
    for k, line in zip(order, lines):
        piece = both[:, at : at + len(line)].reshape(len(both), -1)
        found[k] = piece[:, : leaves[k].size].reshape(-1, *leaves[k].shape)
        at += len(line)
    numbers = iter(range(len(leaves)))
    return jax.tree.map(lambda _: found[next(numbers)], array)


def joined_by_halves(pieces, combine):
    while len(jax.tree.leaves(pieces)[0]) > 1:
        pieces = jax.vmap(combine)(
            *(jax.tree.map(lambda part: part[side::2], pieces) for side in (0, 1))
        )
    return jax.tree.map(lambda part: part[0], pieces)


def prefix(array, axis, combine, identity):
    devices, place = (lax.axis_size(axis), lax.axis_index(axis))
    passed = jnp.arange(devices) < place

    def kept(part, zero, own):
        part = jnp.where(
            passed.reshape(-1, *(1 for _ in own.shape)), part, jnp.asarray(zero, own.dtype)
        )
        return part

    pieces = gathered_once(array, axis)
    return joined_by_halves(jax.tree.map(kept, pieces, identity, array), combine)


def in_blocks(array, dim, devices):
    before, after = (array.shape[:dim], array.shape[dim + 1 :])
    return jnp.moveaxis(array.reshape(*before, devices, -1, *after), dim, 0)


def sum_at_owner(array, axis, dim):
    devices = lax.axis_size(axis)
    tiles = lax.all_to_all(in_blocks(array, dim, devices), axis, 0, 0, tiled=True)
    return jnp.sum(tiles.astype(jnp.float32), axis=0)


def of_everyone(array, axis):
    return copy_for_each(array, axis).sum(axis=0)


def laid_out(tiles, dim):
    tiles = jnp.moveaxis(tiles, 0, dim)
    lengths = tiles.shape
    return tiles.reshape(*lengths[:dim], lengths[dim] * lengths[dim + 1], *lengths[dim + 2 :])


def gather_directly(array, axis, dim):
    tiles = copy_for_each(array, axis)
    return laid_out(tiles, dim)


def moved_by_axis(tiles, axes, order):
    inside = tiles.shape[1:]
    filled = tiles.reshape(*(lax.axis_size(a) for a in axes), *inside)
    for k in order:
        filled = lax.all_to_all(filled, axes[k], k, k, tiled=True)
    return filled.reshape(-1, *inside)


def core_and_chips(array, groups, order, split_dim, concat_dim):
    devices = lax.axis_size(groups[0]) * lax.axis_size(groups[1])
    tiles = in_blocks(array, split_dim, devices)
    return laid_out(moved_by_axis(tiles, groups, order), concat_dim)


def block_pass(carried, block_inputs):
    state_now, decay_before = carried
    decay_log, drive_raw, input_mix, output_mix = block_inputs
    length = decay_log.shape[0]
    cumulative = jnp.cumsum(decay_log, axis=0)
    drive_term = jnp.sqrt(-jnp.expm1(-2.0 * decay_log)) * drive_raw
    pairing = jnp.dot(output_mix, input_mix.T, precision=exact_products)
    causal = jnp.arange(length)[:, None] >= jnp.arange(length)[None, :]
    spread = cumulative[:, None, :] - cumulative[None, :, :]
    kernel = jnp.where(
        causal[:, :, None], jnp.exp(-jnp.where(causal[:, :, None], spread, 0.0)), 0.0
    )
    within = jnp.einsum(
        "tsc,sc->tc", kernel * pairing[:, :, None], drive_term, precision=exact_products
    )
    from_before = jnp.exp(-cumulative) * jnp.dot(output_mix, state_now.T, precision=exact_products)
    remaining = jnp.exp(cumulative - cumulative[-1][None, :])
    state_next = jnp.exp(-cumulative[-1])[:, None] * state_now + jnp.dot(
        (remaining * drive_term).T, input_mix, precision=exact_products
    )
    return (
        (state_next, decay_before + cumulative[-1]),
        (within + from_before, decay_before[None, :] + cumulative),
    )


def join_states(earlier, later):
    return (earlier[0] * later[0], later[0][:, None] * earlier[1] + later[1])


def body(
    conv_x,
    gate_z,
    step,
    decay_rate,
    state_in,
    state_out,
    skip,
    out_weight,
    residual,
    norm_gain,
    expert_ids,
    expert_weights,
):
    token_count, channels = conv_x.shape
    state_size = state_in.shape[1]
    drive_raw = conv_x.astype(jnp.float32)
    decay_log = step.astype(jnp.float32) * decay_rate[None, :]
    block_count = token_count // BLOCK
    shaped = (
        decay_log.reshape(block_count, BLOCK, channels),
        drive_raw.reshape(block_count, BLOCK, channels),
        state_in.reshape(block_count, BLOCK, state_size),
        state_out.reshape(block_count, BLOCK, state_size),
    )
    start_state = (
        jnp.zeros((channels, state_size), jnp.float32),
        jnp.zeros((channels,), jnp.float32),
    )
    (local_state, local_decay), (local_out, running_decay) = lax.scan(
        block_pass, start_state, shaped
    )
    incoming = prefix(
        (jnp.exp(-local_decay), local_state),
        SEQ,
        join_states,
        (jnp.ones((channels,), jnp.float32), jnp.zeros((channels, state_size), jnp.float32)),
    )
    running_decay = running_decay.reshape(token_count, channels)
    scanned = local_out.reshape(token_count, channels) + jnp.exp(-running_decay) * jnp.dot(
        state_out, incoming[1].T, precision=exact_products
    )
    mamba_out = (
        (scanned + skip[None, :] * drive_raw) * jax.nn.silu(gate_z.astype(jnp.float32))
    ).astype(jnp.bfloat16)
    mixer_terms = jnp.dot(mamba_out, out_weight, preferred_element_type=jnp.float32)
    feature_width = D // lax.axis_size("exp")
    share_sum = sum_at_owner(mixer_terms.astype(jnp.bfloat16), ("exp", "ch"), 1)
    share_width = share_sum.shape[1]
    offset = lax.axis_index(("exp", "ch")) * share_width
    stream = (
        lax.dynamic_slice_in_dim(residual, offset, share_width, 1).astype(jnp.float32) + share_sum
    )
    squares = of_everyone(jnp.sum(stream * stream, axis=1), ("exp", "ch"))
    inverse = lax.rsqrt(squares[:, None] / D + norm_epsilon)
    gain_share = lax.dynamic_slice_in_dim(norm_gain, offset, share_width, 0)
    normed_share = (stream * inverse * gain_share[None, :]).astype(jnp.bfloat16)
    normed = gather_directly(normed_share, "ch", 1)
    seq_count = lax.axis_size(SEQ)
    per_owner = max(1, EXPERTS // seq_count)
    group_total = EXPERTS // per_owner
    copies = seq_count // group_total
    slot_count = 9 * token_count // 64
    pair_count = token_count * TOP
    flat_ids = expert_ids.reshape(pair_count)
    onehot = (flat_ids[:, None] == jnp.arange(EXPERTS, dtype=jnp.int32)[None, :]).astype(
        jnp.float32
    )
    strictly = (jnp.arange(pair_count)[:, None] > jnp.arange(pair_count)[None, :]).astype(
        jnp.float32
    )
    earlier = jnp.dot(strictly, onehot, precision=exact_products)
    slot_index = jnp.sum(earlier * onehot, axis=1).astype(jnp.int32)
    targets = (
        flat_ids // per_owner * (slot_count * per_owner)
        + slot_index * per_owner
        + flat_ids % per_owner
    )
    buffer_rows = EXPERTS * slot_count
    selector = jnp.any(
        jnp.arange(buffer_rows, dtype=jnp.int32)[:, None, None]
        == targets.reshape(token_count, TOP)[None, :, :],
        axis=2,
    ).astype(jnp.bfloat16)
    packed = jnp.dot(selector, normed, preferred_element_type=jnp.float32).astype(jnp.bfloat16)
    packed = packed.reshape(group_total, slot_count, per_owner, feature_width)
    outgoing = jnp.tile(packed, (copies, 1, 1, 1))
    arrived = core_and_chips(outgoing, ("seq_0", "seq_1"), (1, 0), 0, 0)
    arrived = arrived.reshape(seq_count * slot_count, per_owner, feature_width)
    mixing = expert_weights.reshape(per_owner, feature_width, expert_weights.shape[-1])
    summed = sum_at_owner(
        jnp.einsum("rjd,jdm->rjm", arrived, mixing, preferred_element_type=jnp.float32).astype(
            jnp.bfloat16
        ),
        "exp",
        0,
    )
    hidden_units = expert_weights.shape[-1] // 2
    hidden = jax.nn.silu(summed[..., :hidden_units]) * summed[..., hidden_units:]
    return hidden.astype(jnp.bfloat16)[None]


def solution(mesh):
    split = Mesh(
        mesh.devices.reshape(16, 2, mesh.shape["exp"], mesh.shape["ch"]),
        ("seq_0", "seq_1", "exp", "ch"),
    )
    in_specs = (
        P(SEQ, ("exp", "ch")),
        P(SEQ, ("exp", "ch")),
        P(SEQ, ("exp", "ch")),
        P(("exp", "ch")),
        P(SEQ, None),
        P(SEQ, None),
        P(("exp", "ch")),
        P(("exp", "ch"), None),
        P(SEQ, None),
        P(),
        P(SEQ, None),
        P(SEQ, None, "exp", "ch", None),
    )
    out_specs = P(SEQ, "exp", None, "ch")
    return jax.shard_map(body, mesh=split, in_specs=in_specs, out_specs=out_specs, check_vma=False)
```

profile of v0, /device:TPU:6, one launch (start us, length us, event | category | flops | bytes accessed | tf_op | source)
XLA Modules:
  0.0 287.0 jit_solution(7772135713714341446)
XLA Ops:
  0.0 1.5 reshape.188
  1.6 1.4 reshape.189
  4.9 22.6 %while.17 = (s32[]{:T(128)}, f32[256,16]{0,1:T(8,128)S(1)}, f32[256]{0:T(256)}, f32[4,32,256]{2,1,0:T(8,128)}, f32[4,32,256]{2,1,0:T(8,128)}, /*index=5*/f32[4,3...) while((s32[]{:T(128)}, f32[256,16]{0,1:T(8,128)S(1)}, ...), condition=%wide.region_4.5_spmd.clone, body=%wide.region_2.4_spmd.clone.sunk | while | flops 5539587 | bytes 682149 | solution.py:163
  6.6 1.2 multiply_reduce_fusion.3
  11.8 1.2 multiply_reduce_fusion.3
  13.1 1.2 fusion.76
  17.6 1.2 multiply_reduce_fusion.3
  23.4 1.2 multiply_reduce_fusion.3
  24.7 1.2 fusion.76
  29.3 19.3 %all-to-all-start = ((f32[32,272,16]{1,2,0:T(8,128)}), f32[32,272,16]{1,2,0:T(8,128)}, u32[]{:S(2)}, u32[]{:S(2)}) async-start(f32[32,272,16]{1,2,0:T(8,128)} %broadcast_in_dim.68), calls=%async_computation | async-start | bytes 1572864 | tf_op jit(solution)/shard_map/all_to_all | solution.py:20
  50.1 1.6 copy.163
  51.8 41.7 %all-to-all-done = f32[32,272,16]{1,2,0:T(8,128)} async-done(((f32[32,272,16]{1,2,0:T(8,128)}), f32[32,272,16]{1,2,0:T(8,128)}, u32[]{:S(2)}, u32[]{:S(2)}) %all-to-all-start) | async-done | bytes 557088 | tf_op jit(solution)/shard_map/all_to_all | solution.py:20
  100.7 1.4 slice_select_fusion
  103.8 1.3 copy.184
  105.2 10.4 %all-to-all-start.1 = ((bf16[32,128,128]{2,1,0:T(8,128)(2,1)}), bf16[32,128,128]{2,1,0:T(8,128)(2,1)}, u32[]{:S(2)}, u32[]{:S(2)}) async-start(bf16[32,128,128]{2,1,0:T(8,128)(2,1)} %bitcast.144), calls=%async_computation.1 | async-start | bytes 2097152 | tf_op jit(solution)/shard_map/all_to_all | solution.py:71
  115.6 26.6 %all-to-all-done.1 = bf16[32,128,128]{2,1,0:T(8,128)(2,1)} async-done(((bf16[32,128,128]{2,1,0:T(8,128)(2,1)}), bf16[32,128,128]{2,1,0:T(8,128)(2,1)}, u32[]{:S(2)}, u32[]{:S(2)}) %all-to-all-start.1) | async-done | bytes 1048608 | tf_op jit(solution)/shard_map/all_to_all | solution.py:71
  142.2 1.4 convert_reduce_fusion.1
  145.1 7.3 %all-to-all-start.2 = ((f32[32,1,128]{2,1,0:T(1,128)}), f32[32,1,128]{2,1,0:T(1,128)S(1)}, u32[]{:S(2)}, u32[]{:S(2)}) async-start(f32[32,1,128]{2,1,0:T(1,128)} %broadcast_in_dim.100), calls=%async_computation.2 | async-start | bytes 32768 | tf_op jit(solution)/shard_map/all_to_all | solution.py:20
  153.2 7.1 %all-to-all-done.2 = f32[32,1,128]{2,1,0:T(1,128)S(1)} async-done(((f32[32,1,128]{2,1,0:T(1,128)}), f32[32,1,128]{2,1,0:T(1,128)S(1)}, u32[]{:S(2)}, u32[]{:S(2)}) %all-to-all-start.2) | async-done | bytes 16416 | tf_op jit(solution)/shard_map/all_to_all | solution.py:20
  162.0 3.4 %all-to-all-start.3 = ((bf16[8,128,128]{1,2,0:T(8,128)(2,1)}), bf16[8,128,128]{1,2,0:T(8,128)(2,1)S(1)}, u32[]{:S(2)}, u32[]{:S(2)}) async-start(bf16[8,128,128]{1,2,0:T(8,128)(2,1)} %broadcast_in_dim.101), calls=%async_computation.3 | async-start | bytes 524288 | tf_op jit(solution)/shard_map/all_to_all | solution.py:20
  166.2 9.6 %all-to-all-done.3 = bf16[8,128,128]{1,2,0:T(8,128)(2,1)S(1)} async-done(((bf16[8,128,128]{1,2,0:T(8,128)(2,1)}), bf16[8,128,128]{1,2,0:T(8,128)(2,1)S(1)}, u32[]{:S(2)}, u32[]{:S(2)}) %all-to-all-start.3) | async-done | bytes 262176 | tf_op jit(solution)/shard_map/all_to_all | solution.py:20
  177.0 2.1 tile.9
  179.1 1.5 copy.168
  181.7 3.6 %tile.11 = bf16[16,2,1,18,1,1024]{5,1,0,3,4,2:T(2,128)(2,1)} reshape(bf16[2,16,18,1024]{3,1,0,2:T(8,128)(2,1)} %tile.10) | data formatting | bytes 2359296 | tf_op jit(solution)/shard_map/tile | solution.py:220
  185.4 1.6 copy.169
  186.9 4.7 %all_to_all.36 = bf16[16,2,1,18,1,1024]{5,0,4,3,2,1:T(8,128)(2,1)S(1)} all-to-all(bf16[16,2,1,18,1,1024]{5,0,4,3,2,1:T(8,128)(2,1)S(1)} %copy.169), channel_id=1, replica_groups=mesh['seq_0'=16,'seq_1'=2,'exp'=4,'ch'=8] {'seq_1'}, dimensions={1} | all-to-all | bytes 2359296 | tf_op jit(solution)/shard_map/all_to_all | solution.py:94
  191.6 1.2 copy.170
  192.8 62.0 %all_to_all.37 = bf16[16,2,1,18,1,1024]{5,1,4,3,2,0:T(2,128)(2,1)S(1)} all-to-all(bf16[16,2,1,18,1,1024]{5,1,4,3,2,0:T(2,128)(2,1)S(1)} %copy.170), channel_id=1, replica_groups=mesh['seq_0'=16,'seq_1'=2,'exp'=4,'ch'=8] {'seq_0'}, dimensions={0} | all-to-all | bytes 2359296 | tf_op jit(solution)/shard_map/all_to_all | solution.py:94
  254.8 1.5 copy.171
  256.4 2.4 reshape.195
  258.7 3.3 %fusion.26 = bf16[576,1536]{1,0:T(8,128)(2,1)S(1)} fusion(bf16[576,1024]{1,0:T(8,128)(2,1)} %reshape.195, bf16[1,1,1024,1,1536]{4,2,3,1,0:T(8,128)(2,1)S(1)} %copy-done), kind=kOutput, calls=%fused_computation.39 | convolution fusion | flops 1812824064 | bytes 6094848 | tf_op jit(solution)/shard_map/rjd,jdm->rjm/dot_general | solution.py:225
  262.0 23.9 %all_to_all.38 = bf16[4,144,1,1536]{3,1,2,0:T(8,128)(2,1)S(1)} all-to-all(bf16[4,144,1,1536]{3,1,2,0:T(8,128)(2,1)S(1)} %bitcast.151), channel_id=1, replica_groups=mesh['seq_0'=16,'seq_1'=2,'exp'=4,'ch'=8] {'exp'}, dimensions={0} | all-to-all | bytes 3538944 | tf_op jit(solution)/shard_map/all_to_all | solution.py:71
  (133 shorter events, 37.1 us)
Async XLA Ops:
  0.0 258.7 %copy-start = (bf16[1,1,1024,1,1536]{4,2,3,1,0:T(8,128)(2,1)S(1)}, bf16[1,1,1024,1,1536]{4,2,3,1,0:T(8,128)(2,1)}, u32[]{:S(2)}) copy-start(bf16[1,1,1024,1,1536]{4,2,3,1,0:T(8,128)(2,1)} %param.25) | copy-start | bytes 9437188
  3.9 1.0 copy-start.2
  27.5 21.1 %copy-start.7 = (bf16[128,256]{1,0:T(8,128)(2,1)S(1)}, bf16[128,256]{1,0:T(8,128)(2,1)}, u32[]{:S(2)}) copy-start(bf16[128,256]{1,0:T(8,128)(2,1)} %param.15) | copy-start | bytes 196612
  27.5 21.8 %copy-start.6 = (f32[4,32,256]{2,1,0:T(8,128)S(1)}, f32[4,32,256]{2,1,0:T(8,128)}, u32[]{:S(2)}) copy-start(f32[4,32,256]{2,1,0:T(8,128)} %get-tuple-element.56) | copy-start | bytes 393220
  29.3 64.2 %all-to-all-start = ((f32[32,272,16]{1,2,0:T(8,128)}), f32[32,272,16]{1,2,0:T(8,128)}, u32[]{:S(2)}, u32[]{:S(2)}) async-start(f32[32,272,16]{1,2,0:T(8,128)} %broadcast_in_dim.68), calls=%async_computation | async-start | bytes 1572864 | tf_op jit(solution)/shard_map/all_to_all | solution.py:20
  51.8 43.6 %copy-start.13 = (pred[32]{0:T(512)(128)(4,1)}, pred[32]{0:T(512)(128)(4,1)S(1)}, u32[]{:S(2)}) copy-start(pred[32]{0:T(512)(128)(4,1)S(1)} %iota_compare_fusion.6) | copy-start | bytes 100
  99.7 3.2 %copy-start.3 = (bf16[128,256]{0,1:T(8,128)(2,1)S(1)}, bf16[128,256]{0,1:T(8,128)(2,1)}, u32[]{:S(2)}) copy-start(bf16[128,256]{0,1:T(8,128)(2,1)} %copy-done.2) | copy-start | bytes 196612
  99.7 3.2 %copy-start.8 = (bf16[128,256]{0,1:T(8,128)(2,1)S(1)}, bf16[128,256]{0,1:T(8,128)(2,1)}, u32[]{:S(2)}) copy-start(bf16[128,256]{0,1:T(8,128)(2,1)} %copy.164) | copy-start | bytes 196612
  100.4 2.4 copy-start.9
  100.4 2.4 copy-start.10
  100.4 2.5 copy-start.4
  100.4 2.5 copy-start.5
  100.4 2.5 copy-start.11
  100.4 2.5 copy-start.14
  100.4 2.9 %copy-start.1 = (bf16[256,4096]{1,0:T(8,128)(2,1)S(1)}, bf16[256,4096]{1,0:T(8,128)(2,1)}, u32[]{:S(2)}) copy-start(bf16[256,4096]{1,0:T(8,128)(2,1)} %param.21) | copy-start | bytes 6291460
  105.2 60.3 %copy-start.12 = (s32[128,2]{0,1:T(2,128)S(1)}, s32[128,2]{0,1:T(2,128)}, u32[]{:S(2)}) copy-start(s32[128,2]{0,1:T(2,128)} %param.24) | copy-start | bytes 3076
  105.2 37.0 %all-to-all-start.1 = ((bf16[32,128,128]{2,1,0:T(8,128)(2,1)}), bf16[32,128,128]{2,1,0:T(8,128)(2,1)}, u32[]{:S(2)}, u32[]{:S(2)}) async-start(bf16[32,128,128]{2,1,0:T(8,128)(2,1)} %bitcast.144), calls=%async_computation.1 | async-start | bytes 2097152 | tf_op jit(solution)/shard_map/all_to_all | solution.py:71
  145.1 15.2 %all-to-all-start.2 = ((f32[32,1,128]{2,1,0:T(1,128)}), f32[32,1,128]{2,1,0:T(1,128)S(1)}, u32[]{:S(2)}, u32[]{:S(2)}) async-start(f32[32,1,128]{2,1,0:T(1,128)} %broadcast_in_dim.100), calls=%async_computation.2 | async-start | bytes 32768 | tf_op jit(solution)/shard_map/all_to_all | solution.py:20
  162.0 13.8 %all-to-all-start.3 = ((bf16[8,128,128]{1,2,0:T(8,128)(2,1)}), bf16[8,128,128]{1,2,0:T(8,128)(2,1)S(1)}, u32[]{:S(2)}, u32[]{:S(2)}) async-start(bf16[8,128,128]{1,2,0:T(8,128)(2,1)} %broadcast_in_dim.101), calls=%async_computation.3 | async-start | bytes 524288 | tf_op jit(solution)/shard_map/all_to_all | solution.py:20
where the time goes:
time: 291 us; the launch traced here: 287 us
  blocking collectives  90.6 us (31%)
  waiting for transfers between devices  85 us (29%)
  starting transfers between devices  40.4 us (14%)
  local copies, waits for them, and re-layouts  37.3 us (13%)
  other arithmetic  22.6 us (8%)
  matrix products  10.3 us (4%)
    all_to_all x2, blocking collectives, moved_by_axis(): filled = lax.all_to_all(filled, axes[k], k, k, tiled=True)  66.7 us
    all_to_all x3, waiting for transfers between devices, copy_for_each(): lax.all_to_all(jnp.broadcast_to(array[None], (devices, *array.shape)), ax...  58.4 us
    all_to_all x3, starting transfers between devices, copy_for_each(): lax.all_to_all(jnp.broadcast_to(array[None], (devices, *array.shape)), ax...  30 us
    all_to_all x1, waiting for transfers between devices, sum_at_owner(): lax.all_to_all(in_blocks(array, dim, devices), axis, 0, 0, tiled=True)  26.6 us
    all_to_all x1, blocking collectives, sum_at_owner(): lax.all_to_all(in_blocks(array, dim, devices), axis, 0, 0, tiled=True)  23.9 us
    all_to_all x1, starting transfers between devices, sum_at_owner(): lax.all_to_all(in_blocks(array, dim, devices), axis, 0, 0, tiled=True)  10.4 us
    another operation x5, local copies, waits for them, and re-layouts, body(): outgoing = jnp.tile(packed, (copies, 1, 1, 1))  9.98 us
  transfers between devices with their start and end apart: 4, of which 4 were waited for; matrix products, arithmetic and copies ran while one was open for 2% of the time, Pallas kernels for 0%

commit v1 on v0

v1 whole, which is shorter than its diff:
```python
import functools

import jax
import jax.numpy as jnp
from jax import lax
from jax.experimental import pallas as pl
from jax.experimental.pallas import tpu as pltpu
from jax.sharding import PartitionSpec as P

MESH = pl.DeviceIdType.MESH
F32 = jnp.float32
BF16 = jnp.bfloat16
EXACT = lax.Precision.HIGHEST
EPSILON = 1e-05
MAIN_SLOTS = 16
TAIL_SLOTS = 2
LANES = 128
STATE_GROUP = 4
NX = 4


def silu(v):
    return v / (1.0 + jnp.exp(-v))


def arrived(ref, sem):
    pltpu.make_async_copy(ref, ref, sem).wait()


def send(src, dst, send_sem, recv_sem, device):
    pltpu.make_async_remote_copy(
        src_ref=src,
        dst_ref=dst,
        send_sem=send_sem,
        recv_sem=recv_sem,
        device_id=device,
        device_id_type=MESH,
    ).start()


def kernel(
    nz,
    ny,
    conv_ref,
    gate_ref,
    step_ref,
    rate_ref,
    b_ref,
    c_ref,
    skip_ref,
    gain_ref,
    ids_ref,
    wout_hbm,
    resid_hbm,
    wexp_hbm,
    out_ref,
    wout,
    resid,
    wexp,
    e_ref,
    d_ref,
    y_ref,
    p_ref,
    s1h,
    s1a,
    s2h,
    s2a,
    inc_h,
    inc_a,
    mx_opp,
    mx_r,
    mx_l,
    mx_rc,
    mx_lc,
    mx_own,
    xo_recv,
    xn_recv,
    ysend,
    yrecv,
    zm_send,
    zt_send,
    zm_recv,
    zt_recv,
    ring,
    lhs,
    pb_opp,
    pb_r,
    pb_l,
    pb_rc,
    pb_lc,
    pb_own,
    po_recv,
    pn_recv,
    sq_send,
    sq_recv,
    local_sem,
    s1_ss,
    s1_rs,
    s2_ss,
    s2_rs,
    xo_ss,
    xo_rs,
    xn_ss,
    xn_rs,
    y_ss,
    y_rs,
    zm_ss,
    zm_rs,
    zt_ss,
    zt_rs,
    ring_ss,
    ring_rs,
    po_ss,
    po_rs,
    pn_ss,
    pn_rs,
    sq_ss,
    sq_rs,
):
    s = lax.axis_index("seq")
    x = lax.axis_index("exp")
    y = lax.axis_index("ch")
    tokens, channels = conv_ref.shape
    features = ny * LANES
    half = tokens // 2
    experts = nz // 2
    xr, xl, xo = lax.rem(x + 1, NX), lax.rem(x + 3, NX), lax.rem(x + 2, NX)
    yr, yl = lax.rem(y + 1, ny), lax.rem(y + ny - 1, ny)

    barrier = pltpu.get_barrier_semaphore()

    @pl.loop(1, nz)
    def _(k):
        pl.semaphore_signal(
            barrier, inc=1, device_id={"seq": lax.rem(s + k, nz)}, device_id_type=MESH
        )

    for k in range(1, NX):
        pl.semaphore_signal(
            barrier, inc=1, device_id={"exp": lax.rem(x + k, NX)}, device_id_type=MESH
        )
    for k in range(1, ny):
        pl.semaphore_signal(
            barrier, inc=1, device_id={"ch": lax.rem(y + k, ny)}, device_id_type=MESH
        )

    share = pl.multiple_of((x * ny + y) * LANES, LANES)
    copy_wout = pltpu.make_async_copy(wout_hbm, wout, local_sem.at[0])
    copy_resid = pltpu.make_async_copy(
        resid_hbm.at[:, pl.ds(share, LANES)], resid, local_sem.at[1]
    )
    copy_wexp = pltpu.make_async_copy(wexp_hbm, wexp, local_sem.at[2])
    copy_wout.start()
    copy_resid.start()
    copy_wexp.start()

    def wide(ref):
        return jnp.concatenate(
            [ref[k : k + 1, :] for k in range(channels // LANES)], axis=1
        )

    conv = conv_ref[...].astype(F32)
    decay_log = step_ref[...].astype(F32) * wide(rate_ref)
    decay = jnp.exp(-decay_log)
    twice = 2.0 * decay_log
    series = twice * (
        1.0
        - twice
        * (
            1.0 / 2.0
            - twice
            * (
                1.0 / 6.0
                - twice * (1.0 / 24.0 - twice * (1.0 / 120.0 - twice * (1.0 / 720.0)))
            )
        )
    )
    lost = jnp.where(twice < 0.25, series, 1.0 - jnp.exp(-twice))
    e_ref[...] = decay
    d_ref[...] = jnp.sqrt(lost) * conv

    def eight_tokens(i, carry):
        state, product, b_now, c_now = carry
        rows = pl.ds(pl.multiple_of(i * 8, 8), 8)
        e8 = e_ref[rows, :]
        d8 = d_ref[rows, :]
        outs, products = [], []
        for k in range(8):
            e1 = e8[k : k + 1, :]
            state = e1 * state + d8[k : k + 1, :] * b_now[:, k : k + 1]
            product = product * e1
            outs.append(jnp.sum(state * c_now[:, k : k + 1], axis=0, keepdims=True))
            products.append(product)
        y_ref[rows, :] = jnp.concatenate(outs, axis=0)
        p_ref[rows, :] = jnp.concatenate(products, axis=0)
        shift = b_now.shape[1] - 8
        return state, product, pltpu.roll(b_now, shift, 1), pltpu.roll(c_now, shift, 1)

    state, product, _, _ = lax.fori_loop(
        0,
        tokens // 8,
        eight_tokens,
        (
            jnp.zeros((b_ref.shape[0], channels), F32),
            jnp.ones((1, channels), F32),
            b_ref[...],
            c_ref[...],
        ),
    )

    group, place = s // STATE_GROUP, lax.rem(s, STATE_GROUP)
    groups = nz // STATE_GROUP
    s1h[place] = state.astype(BF16)
    s1a[place] = product
    pl.semaphore_wait(barrier, nz - 1 + NX - 1 + ny - 1)
    for k in range(1, STATE_GROUP):
        other = lax.rem(place + k, STATE_GROUP)
        device = {"seq": group * STATE_GROUP + other}
        send(s1h.at[place], s1h.at[place], s1_ss.at[0, k], s1_rs.at[0, place], device)
        send(s1a.at[place], s1a.at[place], s1_ss.at[1, k], s1_rs.at[1, place], device)
    gates = silu(gate_ref[...].astype(F32))
    within = y_ref[...] + wide(skip_ref) * conv
    for k in range(1, STATE_GROUP):
        other = lax.rem(place + k, STATE_GROUP)
        arrived(s1h.at[other], s1_rs.at[0, other])
        arrived(s1a.at[other], s1_rs.at[1, other])
    total_h = jnp.zeros_like(state)
    total_a = jnp.ones_like(product)
    before_h = jnp.zeros_like(state)
    before_a = jnp.ones_like(product)
    for j in range(STATE_GROUP):
        h_j = s1h[j].astype(F32)
        a_j = s1a[j]
        total_h = a_j * total_h + h_j
        total_a = a_j * total_a
        earlier = j < place
        before_h = jnp.where(earlier, a_j * before_h + h_j, before_h)
        before_a = jnp.where(earlier, a_j * before_a, before_a)
    s2h[group] = total_h.astype(BF16)
    s2a[group] = total_a
    for k in range(groups - 1, 0, -1):

        @pl.when(group + k < groups)
        def _():
            device = {"seq": s + k * STATE_GROUP}
            send(s2h.at[group], s2h.at[group], s2_ss.at[0, k], s2_rs.at[0, group], device)
            send(s2a.at[group], s2a.at[group], s2_ss.at[1, k], s2_rs.at[1, group], device)

    inc_h[...] = jnp.zeros_like(state)
    for j in range(groups - 1):

        @pl.when(j < group)
        def _():
            arrived(s2h.at[j], s2_rs.at[0, j])
            arrived(s2a.at[j], s2_rs.at[1, j])
            inc_h[...] = s2a[j] * inc_h[...] + s2h[j].astype(F32)

    incoming = before_a * inc_h[...] + before_h

    carried = lax.dot_general(
        c_ref[...], incoming, (((0,), (0,)), ((), ())), precision=EXACT,
        preferred_element_type=F32,
    )
    mamba = ((within + p_ref[...] * carried) * gates).astype(BF16)
    copy_wout.wait()

    def project(which, store):
        @pl.loop(0, ny // 2)
        def _(n):
            start = pl.multiple_of(which * features + n * 2 * LANES, 2 * LANES)
            part = jnp.dot(
                mamba, wout[:, pl.ds(start, 2 * LANES)], preferred_element_type=F32
            )
            for h in range(2):
                for j in range(2):
                    store(
                        h,
                        2 * n + j,
                        part[h * half : (h + 1) * half, j * LANES : (j + 1) * LANES],
                    )

    def into_opp(h, n, v):
        mx_opp[h, n] = v.astype(BF16)

    def into_r(h, n, v):
        if h == 0:
            mx_rc[n] = v
        else:
            mx_r[1, n] = v.astype(BF16)

    def into_l(h, n, v):
        if h == 1:
            mx_lc[n] = v
        else:
            mx_l[0, n] = v.astype(BF16)

    def into_own(h, n, v):
        mx_own[h, n] = v

    to_r, to_l = {"exp": xr}, {"exp": xl}
    project(xo, into_opp)
    send(mx_opp.at[0], xo_recv.at[0], xo_ss.at[0], xo_rs.at[0], to_r)
    send(mx_opp.at[1], xo_recv.at[1], xo_ss.at[1], xo_rs.at[1], to_l)
    project(xr, into_r)
    send(mx_r.at[1], xn_recv.at[0, 1], xn_ss.at[0, 1], xn_rs.at[0, 1], to_r)
    project(xl, into_l)
    send(mx_l.at[0], xn_recv.at[1, 0], xn_ss.at[1, 0], xn_rs.at[1, 0], to_l)
    arrived(xo_recv.at[0], xo_rs.at[0])
    mx_r[0] = (mx_rc[...] + xo_recv[0].astype(F32)).astype(BF16)
    send(mx_r.at[0], xn_recv.at[0, 0], xn_ss.at[0, 0], xn_rs.at[0, 0], to_r)
    arrived(xo_recv.at[1], xo_rs.at[1])
    mx_l[1] = (mx_lc[...] + xo_recv[1].astype(F32)).astype(BF16)
    send(mx_l.at[1], xn_recv.at[1, 1], xn_ss.at[1, 1], xn_rs.at[1, 1], to_l)
    project(xo if NX == 1 else x, into_own)

    wide_experts = max(experts, 16)
    names = lax.broadcasted_iota(jnp.int32, (wide_experts, tokens), 0)
    named = (ids_ref[0:1, :] == names) | (ids_ref[1:2, :] == names)
    count = jnp.where(named, 1.0, 0.0)
    before = jnp.where(
        lax.broadcasted_iota(jnp.int32, (tokens, tokens), 0)
        < lax.broadcasted_iota(jnp.int32, (tokens, tokens), 1),
        1.0,
        0.0,
    )
    earlier = jnp.dot(
        count.astype(BF16), before.astype(BF16), preferred_element_type=F32
    )
    slot = jnp.where(named, earlier, -1.0).astype(BF16)

    def picked(slots, first):
        rows = slots * wide_experts
        spread = jnp.where(
            lax.broadcasted_iota(jnp.int32, (rows, wide_experts), 0) // slots
            == lax.broadcasted_iota(jnp.int32, (rows, wide_experts), 1),
            1.0,
            0.0,
        ).astype(BF16)
        per_row = jnp.dot(spread, slot, preferred_element_type=F32)
        wanted = lax.rem(
            lax.broadcasted_iota(jnp.int32, (rows, tokens), 0), slots
        ).astype(F32) + float(first)
        return jnp.where(per_row == wanted, 1.0, 0.0).astype(BF16)

    pick_main = picked(MAIN_SLOTS, 0)
    pick_tail = picked(TAIL_SLOTS, MAIN_SLOTS)

    for side in range(2):
        for h in (1, 0) if side == 0 else (0, 1):
            arrived(xn_recv.at[side, h], xn_rs.at[side, h])
    for n in range(ny):
        for h in range(2):
            ysend[n, h * half : (h + 1) * half, :] = (
                mx_own[h, n]
                + xn_recv[0, h, n].astype(F32)
                + xn_recv[1, h, n].astype(F32)
            ).astype(BF16)
    for k in range(1, ny):
        other = lax.rem(y + k, ny)
        send(ysend.at[other], yrecv.at[y], y_ss.at[k], y_rs.at[y], {"ch": other})
    yrecv[y] = ysend[y]
    for k in range(1, ny):
        other = lax.rem(y + k, ny)
        arrived(yrecv.at[other], y_rs.at[other])
    copy_resid.wait()
    stream = resid[...].astype(F32)
    for n in range(ny):
        stream = stream + yrecv[n].astype(F32)
    rows_of = stream.astype(BF16)

    main_rows = jnp.dot(pick_main, rows_of, preferred_element_type=F32).astype(BF16)
    tail_rows = jnp.dot(pick_tail, rows_of, preferred_element_type=F32)
    zm_send[...] = main_rows.reshape(wide_experts, MAIN_SLOTS, LANES)
    zt_send[...] = tail_rows.reshape(wide_experts, TAIL_SLOTS, LANES)

    def dispatch(owner):
        expert = lax.rem(owner, experts)
        device = {"seq": owner}
        send(zm_send.at[expert], zm_recv.at[s], zm_ss.at[owner], zm_rs.at[s], device)
        send(zt_send.at[expert], zt_recv.at[s], zt_ss.at[owner], zt_rs.at[s], device)

    dispatch(lax.rem(s + nz // 2, nz))

    @pl.loop(1, nz // 2)
    def _(k):
        far = nz // 2 - k
        dispatch(lax.rem(s + far, nz))
        dispatch(lax.rem(s + nz - far, nz))

    mine = lax.rem(s, experts)
    zm_recv[s] = zm_send[mine]
    zt_recv[s] = zt_send[mine]

    blocks = NX
    sources = nz // blocks
    main = sources * MAIN_SLOTS
    tail = sources * TAIL_SLOTS
    order = [xo, xr, xl, x]
    hops = ny // 2
    even = lax.rem(s, 2) == 0

    def fill(k):
        first = order[k] * sources

        @pl.loop(0, sources)
        def _(j):
            @pl.when(first + j != s)
            def _():
                arrived(zm_recv.at[first + j], zm_rs.at[first + j])
                arrived(zt_recv.at[first + j], zt_rs.at[first + j])

        ring[y, k, 0:main, :] = zm_recv[pl.ds(first, sources)].reshape(main, LANES)
        rest = zt_recv[pl.ds(first, sources)].reshape(tail, LANES)
        if tail < 16:
            rest = jnp.concatenate([rest, jnp.zeros((16 - tail, LANES), F32)], axis=0)
        ring[y, k, main:, :] = rest.astype(BF16)

    def hop_right(k, h, first_part):
        held = lax.rem(y + ny - h + 1, ny)
        got = lax.rem(y + ny - h, ny)
        if first_part:
            send(
                ring.at[held, k], ring.at[held, k], ring_ss.at[0, k, h], ring_rs.at[0, k, h],
                {"ch": yr},
            )
        else:
            arrived(ring.at[got, k], ring_rs.at[0, k, h])

    def hop_left(k, h, first_part):
        held = lax.rem(y + h - 1, ny)
        got = lax.rem(y + h, ny)
        if first_part:
            send(
                ring.at[held, k], ring.at[held, k], ring_ss.at[1, k, h], ring_rs.at[1, k, h],
                {"ch": yl},
            )
        else:
            arrived(ring.at[got, k], ring_rs.at[1, k, h])

    def hop(k, h, first_part):
        if h < hops:
            hop_right(k, h, first_part)
            hop_left(k, h, first_part)
        else:

            @pl.when(even)
            def _():
                hop_right(k, h, first_part)

            @pl.when(jnp.logical_not(even))
            def _():
                hop_left(k, h, first_part)

    gated = pb_own.shape[-1]
    width = 256

    def expert_block(k, store):
        squares = jnp.zeros(lhs.shape[:1] + (LANES,), F32)
        for n in range(ny):
            v = ring[n, k].astype(F32)
            squares = squares + v * v
            lhs[:, n * LANES : (n + 1) * LANES] = (
                v * gain_ref[pl.ds(x * ny + n, 1), :]
            ).astype(BF16)
        sq_send[k] = lax.dot_general(
            jnp.ones((8, LANES), F32), squares, (((1,), (1,)), ((), ())),
            precision=EXACT, preferred_element_type=F32,
        )
        for h in range(2):

            @pl.loop(0, gated // width)
            def _(n):
                start = pl.multiple_of(n * width, width)
                part = jnp.dot(
                    lhs[...],
                    wexp[:, pl.ds(h * gated + start, width)],
                    preferred_element_type=F32,
                )
                store(h, pl.ds(start, width), part)

    def keep_opp(h, at, v):
        pb_opp[h, :, at] = v.astype(BF16)

    def keep_r(h, at, v):
        if h == 0:
            pb_rc[:, at] = v
        else:
            pb_r[1, :, at] = v.astype(BF16)

    def keep_l(h, at, v):
        if h == 1:
            pb_lc[:, at] = v
        else:
            pb_l[0, :, at] = v.astype(BF16)

    def keep_own(h, at, v):
        pb_own[h, :, at] = v

    def after_block(k):
        if k == 0:
            expert_block(0, keep_opp)
            send(pb_opp.at[0], po_recv.at[0], po_ss.at[0], po_rs.at[0], to_r)
            send(pb_opp.at[1], po_recv.at[1], po_ss.at[1], po_rs.at[1], to_l)
            send(sq_send.at[0], sq_recv.at[0], sq_ss.at[0], sq_rs.at[0], {"exp": xo})
        elif k == 1:
            expert_block(1, keep_r)
            send(pb_r.at[1], pn_recv.at[0, 1], pn_ss.at[0, 1], pn_rs.at[0, 1], to_r)
            send(sq_send.at[1], sq_recv.at[1], sq_ss.at[1], sq_rs.at[1], to_r)
            arrived(po_recv.at[0], po_rs.at[0])
            pb_r[0] = (pb_rc[...] + po_recv[0].astype(F32)).astype(BF16)
            send(pb_r.at[0], pn_recv.at[0, 0], pn_ss.at[0, 0], pn_rs.at[0, 0], to_r)
        elif k == 2:
            expert_block(2, keep_l)
            send(pb_l.at[0], pn_recv.at[1, 0], pn_ss.at[1, 0], pn_rs.at[1, 0], to_l)
            send(sq_send.at[2], sq_recv.at[2], sq_ss.at[2], sq_rs.at[2], to_l)
            arrived(po_recv.at[1], po_rs.at[1])
            pb_l[1] = (pb_lc[...] + po_recv[1].astype(F32)).astype(BF16)
            send(pb_l.at[1], pn_recv.at[1, 1], pn_ss.at[1, 1], pn_rs.at[1, 1], to_l)
        else:
            expert_block(3, keep_own)

    for turn in range(blocks + hops):
        for k in range(blocks):
            h = turn - k + 1
            if h == 1:
                fill(k)
            if 1 < h <= hops:
                hop(k, h - 1, False)
            if 1 <= h <= hops:
                hop(k, h, True)
        k = turn - hops
        if 0 <= k < blocks:
            hop(k, hops, False)
            if k == 0:
                copy_wexp.wait()
            after_block(k)

    for k in range(3):
        arrived(sq_recv.at[k], sq_rs.at[k])
    sums = sq_send[3] + sq_recv[0] + sq_recv[1] + sq_recv[2]
    inverse = lax.rsqrt(sums / (NX * features) + EPSILON)
    scale = lax.dot_general(
        inverse, jnp.full((8, LANES), 0.125, F32), (((0,), (0,)), ((), ())),
        precision=EXACT, preferred_element_type=F32,
    )[:, 0:1]
    for side in range(2):
        for h in (1, 0) if side == 0 else (0, 1):
            arrived(pn_recv.at[side, h], pn_rs.at[side, h])
    rows = lhs.shape[0]
    slots = MAIN_SLOTS + TAIL_SLOTS
    final = lax.broadcasted_iota(jnp.int32, (sources * slots, rows), 0)
    place_of = lax.broadcasted_iota(jnp.int32, (sources * slots, rows), 1)
    owner_row, slot_row = final // slots, lax.rem(final, slots)
    taken = jnp.where(
        slot_row < MAIN_SLOTS,
        owner_row * MAIN_SLOTS + slot_row,
        main + owner_row * TAIL_SLOTS + slot_row - MAIN_SLOTS,
    )
    arrange = jnp.where(taken == place_of, 1.0, 0.0).astype(BF16)

    @pl.loop(0, gated // width)
    def _(n):
        at = pl.ds(pl.multiple_of(n * width, width), width)
        both = []
        for h in range(2):
            both.append(
                scale
                * (
                    pb_own[h, :, at]
                    + pn_recv[0, h, :, at].astype(F32)
                    + pn_recv[1, h, :, at].astype(F32)
                )
            )
        hidden = (silu(both[0]) * both[1]).astype(BF16)
        out_ref[:, at] = jnp.dot(arrange, hidden, preferred_element_type=F32).astype(BF16)

    for k in range(1, STATE_GROUP):
        arrived(s1h.at[0], s1_ss.at[0, k])
        arrived(s1a.at[0], s1_ss.at[1, k])
    for k in range(1, groups):

        @pl.when(group + k < groups)
        def _():
            arrived(s2h.at[0], s2_ss.at[0, k])
            arrived(s2a.at[0], s2_ss.at[1, k])

    for h in range(2):
        arrived(mx_opp.at[h], xo_ss.at[h])
        arrived(pb_opp.at[h], po_ss.at[h])
        arrived(mx_r.at[h], xn_ss.at[0, h])
        arrived(mx_l.at[h], xn_ss.at[1, h])
        arrived(pb_r.at[h], pn_ss.at[0, h])
        arrived(pb_l.at[h], pn_ss.at[1, h])
    for k in range(1, ny):
        arrived(ysend.at[0], y_ss.at[k])
    for k in range(3):
        arrived(sq_send.at[k], sq_ss.at[k])

    @pl.loop(1, nz)
    def _(k):
        owner = lax.rem(s + k, nz)
        arrived(zm_send.at[0], zm_ss.at[owner])
        arrived(zt_send.at[0], zt_ss.at[owner])

    for k in range(blocks):
        for h in range(1, hops + 1):
            if h < hops:
                arrived(ring.at[0, k], ring_ss.at[0, k, h])
                arrived(ring.at[0, k], ring_ss.at[1, k, h])
            else:

                @pl.when(even)
                def _():
                    arrived(ring.at[0, k], ring_ss.at[0, k, h])

                @pl.when(jnp.logical_not(even))
                def _():
                    arrived(ring.at[0, k], ring_ss.at[1, k, h])


def body(
    nz,
    ny,
    conv_x,
    gate_z,
    step,
    decay_rate,
    state_in,
    state_out,
    skip,
    out_weight,
    residual,
    norm_gain,
    expert_ids,
    expert_weights,
):
    tokens, channels = conv_x.shape
    entries = state_in.shape[1]
    features = expert_weights.shape[2]
    doubled = expert_weights.shape[-1]
    gated = doubled // 2
    half = tokens // 2
    sources = nz // NX
    tail = max(16, sources * TAIL_SLOTS)
    rows = sources * MAIN_SLOTS + tail
    experts = max(nz // 2, 16)
    hops = ny // 2
    groups = nz // STATE_GROUP
    dma = pltpu.SemaphoreType.DMA
    vmem = pltpu.VMEM
    scratch = [
        vmem(out_weight.shape, BF16),
        vmem((tokens, LANES), BF16),
        vmem((features, doubled), BF16),
        vmem((tokens, channels), F32),
        vmem((tokens, channels), F32),
        vmem((tokens, channels), F32),
        vmem((tokens, channels), F32),
        vmem((STATE_GROUP, entries, channels), BF16),
        vmem((STATE_GROUP, 1, channels), F32),
        vmem((groups, entries, channels), BF16),
        vmem((groups, 1, channels), F32),
        vmem((entries, channels), F32),
        vmem((1, channels), F32),
        vmem((2, ny, half, LANES), BF16),
        vmem((2, ny, half, LANES), BF16),
        vmem((2, ny, half, LANES), BF16),
        vmem((ny, half, LANES), F32),
        vmem((ny, half, LANES), F32),
        vmem((2, ny, half, LANES), F32),
        vmem((2, ny, half, LANES), BF16),
        vmem((2, 2, ny, half, LANES), BF16),
        vmem((ny, tokens, LANES), BF16),
        vmem((ny, tokens, LANES), BF16),
        vmem((experts, MAIN_SLOTS, LANES), BF16),
        vmem((experts, TAIL_SLOTS, LANES), F32),
        vmem((nz, MAIN_SLOTS, LANES), BF16),
        vmem((nz, TAIL_SLOTS, LANES), F32),
        vmem((ny, NX, rows, LANES), BF16),
        vmem((rows, features), BF16),
        vmem((2, rows, gated), BF16),
        vmem((2, rows, gated), BF16),
        vmem((2, rows, gated), BF16),
        vmem((rows, gated), F32),
        vmem((rows, gated), F32),
        vmem((2, rows, gated), F32),
        vmem((2, rows, gated), BF16),
        vmem((2, 2, rows, gated), BF16),
        vmem((NX, 8, rows), F32),
        vmem((NX - 1, 8, rows), F32),
        dma((3,)),
        dma((2, STATE_GROUP)),
        dma((2, STATE_GROUP)),
        dma((2, groups)),
        dma((2, groups)),
        dma((2,)),
        dma((2,)),
        dma((2, 2)),
        dma((2, 2)),
        dma((ny,)),
        dma((ny,)),
        dma((nz,)),
        dma((nz,)),
        dma((nz,)),
        dma((nz,)),
        dma((2, NX, hops + 1)),
        dma((2, NX, hops + 1)),
        dma((2,)),
        dma((2,)),
        dma((2, 2)),
        dma((2, 2)),
        dma((NX - 1,)),
        dma((NX - 1,)),
    ]
    whole = pl.BlockSpec(memory_space=pltpu.VMEM)
    far = pl.BlockSpec(memory_space=pl.ANY)
    out_rows = sources * (MAIN_SLOTS + TAIL_SLOTS)
    hidden = pl.pallas_call(
        functools.partial(kernel, nz, ny),
        out_shape=jax.ShapeDtypeStruct((out_rows, gated), BF16),
        in_specs=[whole] * 9 + [far] * 3,
        out_specs=whole,
        scratch_shapes=scratch,
        compiler_params=pltpu.CompilerParams(collective_id=0, has_side_effects=True),
        name="layer",
    )(
        conv_x,
        gate_z,
        step,
        decay_rate.reshape(channels // LANES, LANES),
        state_in.T,
        state_out.T,
        skip.reshape(channels // LANES, LANES),
        norm_gain.reshape(-1, LANES),
        expert_ids.T,
        out_weight,
        residual,
        expert_weights.reshape(features, doubled),
    )
    return hidden.reshape(1, out_rows, 1, gated)


def solution(mesh):
    in_specs = (
        P("seq", ("exp", "ch")),
        P("seq", ("exp", "ch")),
        P("seq", ("exp", "ch")),
        P(("exp", "ch")),
        P("seq", None),
        P("seq", None),
        P(("exp", "ch")),
        P(("exp", "ch"), None),
        P("seq", None),
        P(),
        P("seq", None),
        P("seq", None, "exp", "ch", None),
    )
    return jax.shard_map(
        functools.partial(body, mesh.shape["seq"], mesh.shape["ch"]),
        mesh=mesh,
        in_specs=in_specs,
        out_specs=P("seq", "exp", None, "ch"),
        check_vma=False,
    )
```

time: 291 us -> 102 us (0.35)
  Pallas kernels: 0 us -> 99 us
  blocking collectives: 90.6 us -> 0 us
  waiting for transfers between devices: 85 us -> 0 us
  starting transfers between devices: 40.4 us -> 0 us
  local copies, waits for them, and re-layouts: 37.3 us -> 1.64 us
  other arithmetic: 22.6 us -> 0 us
  matrix products: 10.3 us -> 0 us
    pallas_call x0 -> x1, Pallas kernels: none -> 99 us  [body(): pl.pallas_call(functools.partial(kernel, nz, ny), out_shape=jax.ShapeDtyp...]
    all_to_all x3 -> x0, blocking collectives: 90.6 us -> none  [the longest x2 66.7 us: moved_by_axis(): filled = lax.all_to_all(filled, axes[k], k, k, tiled=True)]
    all_to_all x4 -> x0, waiting for transfers between devices: 85 us -> none  [the longest x3 58.4 us: copy_for_each(): lax.all_to_all(jnp.broadcast_to(array[None], (devices, *array.shape)), ax...]
    all_to_all x4 -> x0, starting transfers between devices: 40.4 us -> none  [the longest x3 30 us: copy_for_each(): lax.all_to_all(jnp.broadcast_to(array[None], (devices, *array.shape)), ax...]
    another operation x6 -> x0, local copies, waits for them, and re-layouts: 12.4 us -> none  [the longest x5 9.98 us: body(): outgoing = jnp.tile(packed, (copies, 1, 1, 1))]
    dot_general x17 -> x0, matrix products: 10.3 us -> none  [the longest x4 3.35 us: block_pass(): jnp.dot(output_mix, state_now.T, precision=exact_products)]
    slice x18 -> x0, local copies, waits for them, and re-layouts: 6.73 us -> none  [the longest x12 5.58 us: joined_by_halves(): part[side::2]]
    reshape x6 -> x0, local copies, waits for them, and re-layouts: 6.04 us -> none  [the longest x1 1.65 us: body(): local_out.reshape(token_count, channels)]
  transfers between devices with their start and end apart: 4 -> 0, of which waited for: 4 -> 0; matrix products, arithmetic and copies ran while one was open for 2% -> 0% of each run, Pallas kernels for 0% -> 0%
where the time goes in v1:
time: 102 us; the launch traced here: 101 us
  Pallas kernels  99 us (97%)
  local copies, waits for them, and re-layouts  1.64 us (2%)
    pallas_call x1, Pallas kernels, body(): pl.pallas_call(functools.partial(kernel, nz, ny), out_shape=jax.ShapeDtyp...  99 us

profile of v1, /device:TPU:6, one launch (start us, length us, event | category | flops | bytes accessed | tf_op | source)
XLA Modules:
  0.0 100.6 jit_solution(436793396246102316)
XLA Ops:
  0.0 99.0 %layer.1 = bf16[144,768]{1,0:T(8,128)(2,1)} custom-call(bf16[128,256]{1,0:T(8,128)(2,1)} %conv_ref.1, bf16[128,256]{1,0:T(8,128)(2,1)} %gate_ref.1, bf16[128,256]{1,0:T(8,128)(2,1)} %step_ref.1, f32[2,128]{1,0:T(2,128)} %bitcast.13, f32[16,128]{1,0:T(8,128)} %bitcast.11, f32[16,128]{1,0:T(8,128)} %bitcast.12, f32[2,128]{1,0:T(2,128)} %bitcast.14, ...), custom_call_target="tpu_custom_call" | custom-call | tf_op jit(solution)/shard_map/layer/pallas_call | solution.py:718
  99.0 1.6 %copy.14 = bf16[1,144,1,768]{3,1,2,0:T(8,128)(2,1)} copy(bf16[1,144,1,768]{3,1,2,0:T(8,128)(2,1)} %bitcast.9) | data formatting | bytes 442368

commit v2 on v1

v2 whole, which is shorter than its diff:
```python
import functools

import jax
import jax.numpy as jnp
from jax import lax
from jax.experimental import pallas as pl
from jax.experimental.pallas import tpu as pltpu
from jax.sharding import PartitionSpec as P

MESH = pl.DeviceIdType.MESH
F32 = jnp.float32
BF16 = jnp.bfloat16
EXACT = lax.Precision.HIGHEST
EPSILON = 1e-05
MAIN_SLOTS = 16
TAIL_SLOTS = 2
LANES = 128
STATE_GROUP = 4
NX = 4
PARTS = 2


def silu(v):
    return v / (1.0 + jnp.exp(-v))


def arrived(ref, sem):
    pltpu.make_async_copy(ref, ref, sem).wait()


def send(src, dst, send_sem, recv_sem, device):
    pltpu.make_async_remote_copy(
        src_ref=src,
        dst_ref=dst,
        send_sem=send_sem,
        recv_sem=recv_sem,
        device_id=device,
        device_id_type=MESH,
    ).start()


def kernel(
    nz,
    ny,
    conv_ref,
    gate_ref,
    step_ref,
    rate_ref,
    b_ref,
    c_ref,
    skip_ref,
    gain_ref,
    ids_ref,
    wout_hbm,
    resid_hbm,
    wexp_hbm,
    out_ref,
    wout,
    resid,
    wexp,
    e_ref,
    d_ref,
    y_ref,
    p_ref,
    s1h,
    s1a,
    s2h,
    s2a,
    inc_h,
    pick_main,
    pick_tail,
    arrange,
    mx_opp,
    mx_r,
    mx_l,
    mx_rc,
    mx_lc,
    mx_own,
    xo_recv,
    xn_recv,
    ysend,
    yrecv,
    zm_send,
    zt_send,
    zm_recv,
    zt_recv,
    ring,
    lhs,
    squares,
    pb_opp,
    pb_r,
    pb_l,
    pb_rc,
    pb_lc,
    pb_own,
    po_recv,
    pn_recv,
    sq_send,
    sq_recv,
    local_sem,
    s1_ss,
    s1_rs,
    s2_ss,
    s2_rs,
    xo_ss,
    xo_rs,
    xn_ss,
    xn_rs,
    y_ss,
    y_rs,
    zm_ss,
    zm_rs,
    zt_ss,
    zt_rs,
    ring_ss,
    ring_rs,
    po_ss,
    po_rs,
    pn_ss,
    pn_rs,
    sq_ss,
    sq_rs,
):
    s = lax.axis_index("seq")
    x = lax.axis_index("exp")
    y = lax.axis_index("ch")
    tokens, channels = conv_ref.shape
    features = ny * LANES
    part_tokens = tokens // PARTS
    quarter = part_tokens // 2
    experts = nz // 2
    wide_experts = max(experts, 16)
    sources = nz // NX
    main = sources * MAIN_SLOTS
    tail = sources * TAIL_SLOTS
    block_rows = lhs.shape[1]
    xr, xl, xo = lax.rem(x + 1, NX), lax.rem(x + 3, NX), lax.rem(x + 2, NX)
    yr, yl = lax.rem(y + 1, ny), lax.rem(y + ny - 1, ny)

    barrier = pltpu.get_barrier_semaphore()

    @pl.loop(1, nz)
    def _(k):
        pl.semaphore_signal(
            barrier, inc=1, device_id={"seq": lax.rem(s + k, nz)}, device_id_type=MESH
        )

    for k in range(1, NX):
        pl.semaphore_signal(
            barrier, inc=1, device_id={"exp": lax.rem(x + k, NX)}, device_id_type=MESH
        )
    for k in range(1, ny):
        pl.semaphore_signal(
            barrier, inc=1, device_id={"ch": lax.rem(y + k, ny)}, device_id_type=MESH
        )

    share = pl.multiple_of((x * ny + y) * LANES, LANES)
    copy_wout = pltpu.make_async_copy(wout_hbm, wout, local_sem.at[0])
    copy_resid = pltpu.make_async_copy(
        resid_hbm.at[:, pl.ds(share, LANES)], resid, local_sem.at[1]
    )
    copy_wexp = pltpu.make_async_copy(wexp_hbm, wexp, local_sem.at[2])
    copy_wout.start()
    copy_resid.start()
    copy_wexp.start()

    def wide(ref):
        return jnp.concatenate(
            [ref[k : k + 1, :] for k in range(channels // LANES)], axis=1
        )

    conv = conv_ref[...].astype(F32)
    decay_log = step_ref[...].astype(F32) * wide(rate_ref)
    decay = jnp.exp(-decay_log)
    twice = 2.0 * decay_log
    series = twice * (
        1.0
        - twice
        * (
            1.0 / 2.0
            - twice
            * (
                1.0 / 6.0
                - twice * (1.0 / 24.0 - twice * (1.0 / 120.0 - twice * (1.0 / 720.0)))
            )
        )
    )
    lost = jnp.where(twice < 0.25, series, 1.0 - jnp.exp(-twice))
    e_ref[...] = decay
    d_ref[...] = jnp.sqrt(lost) * conv

    def eight_tokens(i, carry):
        state, product, b_now, c_now = carry
        rows = pl.ds(pl.multiple_of(i * 8, 8), 8)
        e8 = e_ref[rows, :]
        d8 = d_ref[rows, :]
        outs, products = [], []
        for k in range(8):
            e1 = e8[k : k + 1, :]
            state = e1 * state + d8[k : k + 1, :] * b_now[:, k : k + 1]
            product = product * e1
            outs.append(jnp.sum(state * c_now[:, k : k + 1], axis=0, keepdims=True))
            products.append(product)
        y_ref[rows, :] = jnp.concatenate(outs, axis=0)
        p_ref[rows, :] = jnp.concatenate(products, axis=0)
        shift = b_now.shape[1] - 8
        return state, product, pltpu.roll(b_now, shift, 1), pltpu.roll(c_now, shift, 1)

    state, product, _, _ = lax.fori_loop(
        0,
        tokens // 8,
        eight_tokens,
        (
            jnp.zeros((b_ref.shape[0], channels), F32),
            jnp.ones((1, channels), F32),
            b_ref[...],
            c_ref[...],
        ),
    )

    group, place = s // STATE_GROUP, lax.rem(s, STATE_GROUP)
    groups = nz // STATE_GROUP
    s1h[place] = state.astype(BF16)
    s1a[place] = product
    pl.semaphore_wait(barrier, nz - 1 + NX - 1 + ny - 1)
    for k in range(1, STATE_GROUP):
        other = lax.rem(place + k, STATE_GROUP)
        device = {"seq": group * STATE_GROUP + other}
        send(s1h.at[place], s1h.at[place], s1_ss.at[0], s1_rs.at[0], device)
        send(s1a.at[place], s1a.at[place], s1_ss.at[1], s1_rs.at[1], device)
    gates = silu(gate_ref[...].astype(F32))
    within = y_ref[...] + wide(skip_ref) * conv
    arrived(s1h.at[pl.ds(0, STATE_GROUP - 1)], s1_rs.at[0])
    arrived(s1a.at[pl.ds(0, STATE_GROUP - 1)], s1_rs.at[1])
    total_h = jnp.zeros_like(state)
    total_a = jnp.ones_like(product)
    before_h = jnp.zeros_like(state)
    before_a = jnp.ones_like(product)
    for j in range(STATE_GROUP):
        h_j = s1h[j].astype(F32)
        a_j = s1a[j]
        total_h = a_j * total_h + h_j
        total_a = a_j * total_a
        earlier = j < place
        before_h = jnp.where(earlier, a_j * before_h + h_j, before_h)
        before_a = jnp.where(earlier, a_j * before_a, before_a)
    s2h[group] = total_h.astype(BF16)
    s2a[group] = total_a
    for k in range(groups - 1, 0, -1):

        @pl.when(group + k < groups)
        def _():
            device = {"seq": s + k * STATE_GROUP}
            send(s2h.at[group], s2h.at[group], s2_ss.at[0, k], s2_rs.at[0, group], device)
            send(s2a.at[group], s2a.at[group], s2_ss.at[1, k], s2_rs.at[1, group], device)

    names = lax.broadcasted_iota(jnp.int32, (wide_experts, tokens), 0)
    named = (ids_ref[0:1, :] == names) | (ids_ref[1:2, :] == names)
    count = jnp.where(named, 1.0, 0.0)
    before = jnp.where(
        lax.broadcasted_iota(jnp.int32, (tokens, tokens), 0)
        < lax.broadcasted_iota(jnp.int32, (tokens, tokens), 1),
        1.0,
        0.0,
    )
    earlier = jnp.dot(
        count.astype(BF16), before.astype(BF16), preferred_element_type=F32
    )
    slot = jnp.where(named, earlier, -1.0).astype(BF16)

    def picked(slots, first):
        rows = slots * wide_experts
        spread = jnp.where(
            lax.broadcasted_iota(jnp.int32, (rows, wide_experts), 0) // slots
            == lax.broadcasted_iota(jnp.int32, (rows, wide_experts), 1),
            1.0,
            0.0,
        ).astype(BF16)
        per_row = jnp.dot(spread, slot, preferred_element_type=F32)
        wanted = lax.rem(
            lax.broadcasted_iota(jnp.int32, (rows, tokens), 0), slots
        ).astype(F32) + float(first)
        return jnp.where(per_row == wanted, 1.0, 0.0).astype(BF16)

    pick_main[...] = picked(MAIN_SLOTS, 0)
    pick_tail[...] = picked(TAIL_SLOTS, MAIN_SLOTS)
    slots = MAIN_SLOTS + TAIL_SLOTS
    final = lax.broadcasted_iota(jnp.int32, (sources * slots, block_rows), 0)
    place_of = lax.broadcasted_iota(jnp.int32, (sources * slots, block_rows), 1)
    owner_row, slot_row = final // slots, lax.rem(final, slots)
    taken = jnp.where(
        slot_row < MAIN_SLOTS,
        owner_row * MAIN_SLOTS + slot_row,
        main + owner_row * TAIL_SLOTS + slot_row - MAIN_SLOTS,
    )
    arrange[...] = jnp.where(taken == place_of, 1.0, 0.0).astype(BF16)

    inc_h[...] = jnp.zeros_like(state)
    for j in range(groups - 1):

        @pl.when(j < group)
        def _():
            arrived(s2h.at[j], s2_rs.at[0, j])
            arrived(s2a.at[j], s2_rs.at[1, j])
            inc_h[...] = s2a[j] * inc_h[...] + s2h[j].astype(F32)

    incoming = before_a * inc_h[...] + before_h

    carried = lax.dot_general(
        c_ref[...], incoming, (((0,), (0,)), ((), ())), precision=EXACT,
        preferred_element_type=F32,
    )
    mamba = ((within + p_ref[...] * carried) * gates).astype(BF16)
    copy_wout.wait()

    def project(which, store):
        @pl.loop(0, ny // 2)
        def _(n):
            start = pl.multiple_of(which * features + n * 2 * LANES, 2 * LANES)
            part = jnp.dot(
                mamba, wout[:, pl.ds(start, 2 * LANES)], preferred_element_type=F32
            )
            for q in range(PARTS):
                for h in range(2):
                    first = q * part_tokens + h * quarter
                    for j in range(2):
                        store(
                            q,
                            h,
                            2 * n + j,
                            part[first : first + quarter, j * LANES : (j + 1) * LANES],
                        )

    def into_opp(q, h, n, v):
        mx_opp[q, h, n] = v.astype(BF16)

    def into_r(q, h, n, v):
        if h == 0:
            mx_rc[q, n] = v
        else:
            mx_r[q, 1, n] = v.astype(BF16)

    def into_l(q, h, n, v):
        if h == 1:
            mx_lc[q, n] = v
        else:
            mx_l[q, 0, n] = v.astype(BF16)

    def into_own(q, h, n, v):
        mx_own[q, h, n] = v

    to_r, to_l = {"exp": xr}, {"exp": xl}

    def pass_on(side, q, h):
        held, device = (mx_r, to_r) if side == 0 else (mx_l, to_l)
        send(
            held.at[q, h], xn_recv.at[side, q, h], xn_ss.at[side, q, h],
            xn_rs.at[side, q, h], device,
        )

    def add_and_pass_on(q):
        arrived(xo_recv.at[q, 0], xo_rs.at[q, 0])
        mx_r[q, 0] = (mx_rc[q] + xo_recv[q, 0].astype(F32)).astype(BF16)
        pass_on(0, q, 0)
        arrived(xo_recv.at[q, 1], xo_rs.at[q, 1])
        mx_l[q, 1] = (mx_lc[q] + xo_recv[q, 1].astype(F32)).astype(BF16)
        pass_on(1, q, 1)

    project(xo, into_opp)
    for q in range(PARTS):
        send(mx_opp.at[q, 0], xo_recv.at[q, 0], xo_ss.at[q, 0], xo_rs.at[q, 0], to_r)
        send(mx_opp.at[q, 1], xo_recv.at[q, 1], xo_ss.at[q, 1], xo_rs.at[q, 1], to_l)
    project(xr, into_r)
    pass_on(0, 0, 1)
    project(xl, into_l)
    pass_on(1, 0, 0)
    for q in range(PARTS):
        add_and_pass_on(q)
        if q + 1 < PARTS:
            pass_on(0, q + 1, 1)
            pass_on(1, q + 1, 0)
        if q == 0:
            project(x, into_own)

    far_first = sorted(range(1, ny), key=lambda k: -min(k, ny - k))
    for q in range(PARTS):
        for side in range(2):
            for h in (1, 0) if side == 0 else (0, 1):
                arrived(xn_recv.at[side, q, h], xn_rs.at[side, q, h])
        for n in range(ny):
            for h in range(2):
                ysend[q, n, h * quarter : (h + 1) * quarter, :] = (
                    mx_own[q, h, n]
                    + xn_recv[0, q, h, n].astype(F32)
                    + xn_recv[1, q, h, n].astype(F32)
                ).astype(BF16)
        for k in far_first:
            other = lax.rem(y + k, ny)
            send(
                ysend.at[q, other], yrecv.at[q, y], y_ss.at[q], y_rs.at[q],
                {"ch": other},
            )
        yrecv[q, y] = ysend[q, y]
    copy_resid.wait()
    streams = []
    for q in range(PARTS):
        arrived(yrecv.at[q, pl.ds(0, ny - 1)], y_rs.at[q])
        stream = resid[q * part_tokens : (q + 1) * part_tokens, :].astype(F32)
        for n in range(ny):
            stream = stream + yrecv[q, n].astype(F32)
        streams.append(stream)
    rows_of = jnp.concatenate(streams, axis=0).astype(BF16)

    main_rows = jnp.dot(pick_main[...], rows_of, preferred_element_type=F32).astype(BF16)
    tail_rows = jnp.dot(pick_tail[...], rows_of, preferred_element_type=F32)
    zm_send[...] = main_rows.reshape(wide_experts, MAIN_SLOTS, LANES)
    zt_send[...] = tail_rows.reshape(wide_experts, TAIL_SLOTS, LANES)

    def dispatch(owner):
        expert = lax.rem(owner, experts)
        device = {"seq": owner}
        send(zm_send.at[expert], zm_recv.at[s], zm_ss, zm_rs.at[s // sources], device)
        send(zt_send.at[expert], zt_recv.at[s], zt_ss, zt_rs.at[s // sources], device)

    dispatch(lax.rem(s + nz // 2, nz))

    @pl.loop(1, nz // 2)
    def _(k):
        far = nz // 2 - k
        dispatch(lax.rem(s + far, nz))
        dispatch(lax.rem(s + nz - far, nz))

    mine = lax.rem(s, experts)
    zm_recv[s] = zm_send[mine]
    zt_recv[s] = zt_send[mine]

    blocks = NX
    order = [xo, xr, xl, x]
    hops = ny // 2
    even = lax.rem(s, 2) == 0

    def fill(k):
        first = order[k] * sources

        def all_of(number):
            arrived(zm_recv.at[pl.ds(0, number)], zm_rs.at[order[k]])
            arrived(zt_recv.at[pl.ds(0, number)], zt_rs.at[order[k]])

        @pl.when(s // sources == order[k])
        def _():
            all_of(sources - 1)

        @pl.when(s // sources != order[k])
        def _():
            all_of(sources)

        ring[y, k, 0:main, :] = zm_recv[pl.ds(first, sources)].reshape(main, LANES)
        rest = zt_recv[pl.ds(first, sources)].reshape(tail, LANES)
        if tail < 16:
            rest = jnp.concatenate([rest, jnp.zeros((16 - tail, LANES), F32)], axis=0)
        ring[y, k, main:, :] = rest.astype(BF16)

    def hop_right(k, h, first_part):
        held = lax.rem(y + ny - h + 1, ny)
        got = lax.rem(y + ny - h, ny)
        if first_part:
            send(
                ring.at[held, k], ring.at[held, k], ring_ss, ring_rs.at[0, k, h - 1],
                {"ch": yr},
            )
        else:
            arrived(ring.at[got, k], ring_rs.at[0, k, h - 1])

    def hop_left(k, h, first_part):
        held = lax.rem(y + h - 1, ny)
        got = lax.rem(y + h, ny)
        if first_part:
            send(
                ring.at[held, k], ring.at[held, k], ring_ss, ring_rs.at[1, k, h - 1],
                {"ch": yl},
            )
        else:
            arrived(ring.at[got, k], ring_rs.at[1, k, h - 1])

    def hop(k, h, first_part):
        if h < hops:
            hop_right(k, h, first_part)
            hop_left(k, h, first_part)
        else:

            @pl.when(even)
            def _():
                hop_right(k, h, first_part)

            @pl.when(jnp.logical_not(even))
            def _():
                hop_left(k, h, first_part)

    gated = pb_own.shape[-1]
    width = 256

    def prepare(k, n, first):
        v = ring[n, k].astype(F32)
        squares[k] = v * v if first else squares[k] + v * v
        at = pl.ds(pl.multiple_of(n * LANES, LANES), LANES)
        lhs[k, :, at] = (v * gain_ref[pl.ds(x * ny + n, 1), :]).astype(BF16)

    def expert_half(k, h, store):
        @pl.loop(0, gated // width)
        def _(n):
            start = pl.multiple_of(n * width, width)
            column = pl.multiple_of(h * gated + n * width, width)
            part = jnp.dot(
                lhs[k], wexp[:, pl.ds(column, width)], preferred_element_type=F32
            )
            store(h, pl.ds(start, width), part)

    def square_sums(k):
        sq_send[k] = lax.dot_general(
            jnp.ones((8, LANES), F32), squares[k], (((1,), (1,)), ((), ())),
            precision=EXACT, preferred_element_type=F32,
        )

    def keep_opp(h, at, v):
        pb_opp[h, :, at] = v.astype(BF16)

    def keep_r(h, at, v):
        if h == 0:
            pb_rc[:, at] = v
        else:
            pb_r[1, :, at] = v.astype(BF16)

    def keep_l(h, at, v):
        if h == 1:
            pb_lc[:, at] = v
        else:
            pb_l[0, :, at] = v.astype(BF16)

    def keep_own(h, at, v):
        pb_own[h, :, at] = v

    def all_left():
        arrived(s1h.at[pl.ds(0, STATE_GROUP - 1)], s1_ss.at[0])
        arrived(s1a.at[pl.ds(0, STATE_GROUP - 1)], s1_ss.at[1])
        for k in range(1, groups):

            @pl.when(group + k < groups)
            def _():
                arrived(s2h.at[0], s2_ss.at[0, k])
                arrived(s2a.at[0], s2_ss.at[1, k])

        for h in range(2):
            for q in range(PARTS):
                arrived(mx_opp.at[q, h], xo_ss.at[q, h])
                arrived(mx_r.at[q, h], xn_ss.at[0, q, h])
                arrived(mx_l.at[q, h], xn_ss.at[1, q, h])
            arrived(pb_opp.at[h], po_ss.at[h])
        arrived(pb_r.at[1], pn_ss.at[0, 1])
        arrived(pb_l.at[0], pn_ss.at[1, 0])
        for q in range(PARTS):
            arrived(ysend.at[q, pl.ds(0, ny - 1)], y_ss.at[q])
        for k in range(3):
            arrived(sq_send.at[k], sq_ss.at[k])

        arrived(zm_recv.at[pl.ds(0, nz - 1)], zm_ss)
        arrived(zt_recv.at[pl.ds(0, nz - 1)], zt_ss)
        arrived(ring.at[pl.ds(0, ny - 1)], ring_ss)

    def exchange(k, h):
        if h == 1:
            fill(k)
        else:
            hop(k, h - 1, False)
        if h <= hops:
            hop(k, h, True)
        if h == 1:
            prepare(k, y, True)
        else:
            prepare(k, lax.rem(y + h - 1, ny), False)
            if h <= hops:
                prepare(k, lax.rem(y + ny - h + 1, ny), False)

    def opposite_block():
        exchange(0, hops + 1)
        copy_wexp.wait()
        for turn in range(2):
            h = jnp.where(even, turn, 1 - turn)
            expert_half(0, h, keep_opp)
            device = {"exp": jnp.where(h == 0, xr, xl)}
            send(pb_opp.at[h], po_recv.at[h], po_ss.at[h], po_rs.at[h], device)

    at_turn = ((3, 6, 9, 12), (4, 7.5, 13, 16), (5, 10, 14, 17), (7, 11, 15, 18))
    turns = sorted(
        (at_turn[k][h - 1], k, h) for k in range(blocks) for h in range(1, hops + 1)
    )
    first_done = max(i for i, (_, k, _) in enumerate(turns) if k == 0)
    for i, (_, k, h) in enumerate(turns):
        exchange(k, h)
        if i == min(first_done + 3, len(turns) - 1):
            opposite_block()
    exchange(1, hops + 1)
    expert_half(1, 1, keep_r)
    send(pb_r.at[1], pn_recv.at[0, 1], pn_ss.at[0, 1], pn_rs.at[0, 1], to_r)
    exchange(2, hops + 1)
    expert_half(2, 0, keep_l)
    send(pb_l.at[0], pn_recv.at[1, 0], pn_ss.at[1, 0], pn_rs.at[1, 0], to_l)
    for k, device in enumerate(({"exp": xo}, to_r, to_l)):
        square_sums(k)
        send(sq_send.at[k], sq_recv.at[k], sq_ss.at[k], sq_rs.at[k], device)
    expert_half(1, 0, keep_r)
    expert_half(2, 1, keep_l)
    exchange(3, hops + 1)
    square_sums(3)
    for h in range(2):
        expert_half(3, h, keep_own)
    arrived(po_recv.at[0], po_rs.at[0])
    pb_r[0] = (pb_rc[...] + po_recv[0].astype(F32)).astype(BF16)
    send(pb_r.at[0], pn_recv.at[0, 0], pn_ss.at[0, 0], pn_rs.at[0, 0], to_r)
    arrived(po_recv.at[1], po_rs.at[1])
    pb_l[1] = (pb_lc[...] + po_recv[1].astype(F32)).astype(BF16)
    send(pb_l.at[1], pn_recv.at[1, 1], pn_ss.at[1, 1], pn_rs.at[1, 1], to_l)

    all_left()
    for k in range(3):
        arrived(sq_recv.at[k], sq_rs.at[k])
    sums = sq_send[3] + sq_recv[0] + sq_recv[1] + sq_recv[2]
    inverse = lax.rsqrt(sums / (NX * features) + EPSILON)
    scale = lax.dot_general(
        inverse, jnp.full((8, LANES), 0.125, F32), (((0,), (0,)), ((), ())),
        precision=EXACT, preferred_element_type=F32,
    )
    scale = jnp.concatenate([scale] * (width // LANES), axis=1)
    arrived(pn_recv.at[0, 1], pn_rs.at[0, 1])
    pb_own[1] = pb_own[1] + pn_recv[0, 1].astype(F32)
    arrived(pn_recv.at[1, 0], pn_rs.at[1, 0])
    pb_own[0] = pb_own[0] + pn_recv[1, 0].astype(F32)
    arrived(pn_recv.at[0, 0], pn_rs.at[0, 0])
    arrived(pn_recv.at[1, 1], pn_rs.at[1, 1])

    @pl.loop(0, gated // width)
    def _(n):
        at = pl.ds(pl.multiple_of(n * width, width), width)
        gate_part = scale * (pb_own[0, :, at] + pn_recv[0, 0, :, at].astype(F32))
        up_part = scale * (pb_own[1, :, at] + pn_recv[1, 1, :, at].astype(F32))
        hidden = (silu(gate_part) * up_part).astype(BF16)
        out_ref[:, at] = jnp.dot(
            arrange[...], hidden, preferred_element_type=F32
        ).astype(BF16)

    arrived(pb_r.at[0], pn_ss.at[0, 0])
    arrived(pb_l.at[1], pn_ss.at[1, 1])


def body(
    nz,
    ny,
    conv_x,
    gate_z,
    step,
    decay_rate,
    state_in,
    state_out,
    skip,
    out_weight,
    residual,
    norm_gain,
    expert_ids,
    expert_weights,
):
    tokens, channels = conv_x.shape
    entries = state_in.shape[1]
    features = expert_weights.shape[2]
    doubled = expert_weights.shape[-1]
    gated = doubled // 2
    part_tokens = tokens // PARTS
    quarter = part_tokens // 2
    sources = nz // NX
    tail = max(16, sources * TAIL_SLOTS)
    rows = sources * MAIN_SLOTS + tail
    experts = max(nz // 2, 16)
    hops = ny // 2
    groups = nz // STATE_GROUP
    dma = pltpu.SemaphoreType.DMA
    vmem = pltpu.VMEM
    scratch = [
        vmem(out_weight.shape, BF16),
        vmem((tokens, LANES), BF16),
        vmem((features, doubled), BF16),
        vmem((tokens, channels), F32),
        vmem((tokens, channels), F32),
        vmem((tokens, channels), F32),
        vmem((tokens, channels), F32),
        vmem((STATE_GROUP, entries, channels), BF16),
        vmem((STATE_GROUP, 1, channels), F32),
        vmem((groups, entries, channels), BF16),
        vmem((groups, 1, channels), F32),
        vmem((entries, channels), F32),
        vmem((MAIN_SLOTS * experts, tokens), BF16),
        vmem((TAIL_SLOTS * experts, tokens), BF16),
        vmem((sources * (MAIN_SLOTS + TAIL_SLOTS), rows), BF16),
        vmem((PARTS, 2, ny, quarter, LANES), BF16),
        vmem((PARTS, 2, ny, quarter, LANES), BF16),
        vmem((PARTS, 2, ny, quarter, LANES), BF16),
        vmem((PARTS, ny, quarter, LANES), F32),
        vmem((PARTS, ny, quarter, LANES), F32),
        vmem((PARTS, 2, ny, quarter, LANES), F32),
        vmem((PARTS, 2, ny, quarter, LANES), BF16),
        vmem((2, PARTS, 2, ny, quarter, LANES), BF16),
        vmem((PARTS, ny, part_tokens, LANES), BF16),
        vmem((PARTS, ny, part_tokens, LANES), BF16),
        vmem((experts, MAIN_SLOTS, LANES), BF16),
        vmem((experts, TAIL_SLOTS, LANES), F32),
        vmem((nz, MAIN_SLOTS, LANES), BF16),
        vmem((nz, TAIL_SLOTS, LANES), F32),
        vmem((ny, NX, rows, LANES), BF16),
        vmem((NX, rows, features), BF16),
        vmem((NX, rows, LANES), F32),
        vmem((2, rows, gated), BF16),
        vmem((2, rows, gated), BF16),
        vmem((2, rows, gated), BF16),
        vmem((rows, gated), F32),
        vmem((rows, gated), F32),
        vmem((2, rows, gated), F32),
        vmem((2, rows, gated), BF16),
        vmem((2, 2, rows, gated), BF16),
        vmem((NX, 8, rows), F32),
        vmem((NX - 1, 8, rows), F32),
        dma((3,)),
        dma((2,)),
        dma((2,)),
        dma((2, groups)),
        dma((2, groups)),
        dma((PARTS, 2)),
        dma((PARTS, 2)),
        dma((2, PARTS, 2)),
        dma((2, PARTS, 2)),
        dma((PARTS,)),
        dma((PARTS,)),
        dma,
        dma((NX,)),
        dma,
        dma((NX,)),
        dma,
        dma((2, NX, hops)),
        dma((2,)),
        dma((2,)),
        dma((2, 2)),
        dma((2, 2)),
        dma((NX - 1,)),
        dma((NX - 1,)),
    ]
    whole = pl.BlockSpec(memory_space=pltpu.VMEM)
    far = pl.BlockSpec(memory_space=pl.ANY)
    out_rows = sources * (MAIN_SLOTS + TAIL_SLOTS)
    hidden = pl.pallas_call(
        functools.partial(kernel, nz, ny),
        out_shape=pltpu.VMEM((out_rows, gated), BF16),
        in_specs=[whole] * 9 + [far] * 3,
        out_specs=whole,
        scratch_shapes=scratch,
        compiler_params=pltpu.CompilerParams(collective_id=0, has_side_effects=True),
        name="layer",
    )(
        conv_x,
        gate_z,
        step,
        decay_rate.reshape(channels // LANES, LANES),
        state_in.T,
        state_out.T,
        skip.reshape(channels // LANES, LANES),
        norm_gain.reshape(-1, LANES),
        expert_ids.T,
        out_weight,
        residual,
        expert_weights.reshape(features, doubled),
    )
    return hidden.reshape(1, out_rows, 1, gated)


def solution(mesh):
    in_specs = (
        P("seq", ("exp", "ch")),
        P("seq", ("exp", "ch")),
        P("seq", ("exp", "ch")),
        P(("exp", "ch")),
        P("seq", None),
        P("seq", None),
        P(("exp", "ch")),
        P(("exp", "ch"), None),
        P("seq", None),
        P(),
        P("seq", None),
        P("seq", None, "exp", "ch", None),
    )
    return jax.shard_map(
        functools.partial(body, mesh.shape["seq"], mesh.shape["ch"]),
        mesh=mesh,
        in_specs=in_specs,
        out_specs=P("seq", "exp", None, "ch"),
        check_vma=False,
    )
```

time: 102 us -> 92.6 us (0.908); the launches traced: 101 us -> 92.4 us
  Pallas kernels: 99 us -> 91.7 us
    pallas_call x1, Pallas kernels: 99 us -> 91.7 us  [body(): pl.pallas_call(functools.partial(kernel, nz, ny), out_shape=pltpu.VMEM((o...]
where the time goes in v2:
time: 92.6 us; the launch traced here: 92.4 us
  Pallas kernels  91.7 us (99%)
    pallas_call x1, Pallas kernels, body(): pl.pallas_call(functools.partial(kernel, nz, ny), out_shape=pltpu.VMEM((o...  91.7 us

profile of v2, /device:TPU:6, one launch (start us, length us, event | category | flops | bytes accessed | tf_op | source)
XLA Modules:
  0.0 92.4 jit_solution(12559985891796574453)
XLA Ops:
  0.0 91.7 %layer.1 = bf16[144,768]{1,0:T(8,128)(2,1)S(1)} custom-call(bf16[128,256]{1,0:T(8,128)(2,1)} %conv_ref.1, bf16[128,256]{1,0:T(8,128)(2,1)} %gate_ref.1, bf16[128,256]{1,0:T(8,128)(2,1)} %step_ref.1, f32[2,128]{1,0:T(2,128)} %bitcast.13, f32[16,128]{1,0:T(8,128)} %bitcast.11, f32[16,128]{1,0:T(8,128)} %bitcast.12, f32[2,128]{1,0:T(2,128)} %bitcast.14, ...), custom_call_target="tpu_custom_call" | custom-call | tf_op jit(solution)/shard_map/layer/pallas_call | solution.py:755
  91.7 0.7 copy.14

commit v3 on v2

--- a/solution.py
+++ b/solution.py
@@ -17,7 +17,7 @@
 LANES = 128
 STATE_GROUP = 4
 NX = 4
-PARTS = 2
+PARTS = 4
 
 
 def silu(v):
@@ -42,6 +42,19 @@
 def kernel(
     nz,
     ny,
+    conv_hbm,
+    gate_hbm,
+    step_hbm,
+    rate_hbm,
+    b_hbm,
+    c_hbm,
+    skip_hbm,
+    gain_hbm,
+    ids_hbm,
+    wout_hbm,
+    resid_hbm,
+    wexp_hbm,
+    out_ref,
     conv_ref,
     gate_ref,
     step_ref,
@@ -51,10 +64,6 @@
     skip_ref,
     gain_ref,
     ids_ref,
-    wout_hbm,
-    resid_hbm,
-    wexp_hbm,
-    out_ref,
     wout,
     resid,
     wexp,
@@ -124,7 +133,7 @@
     s = lax.axis_index("seq")
     x = lax.axis_index("exp")
     y = lax.axis_index("ch")
-    tokens, channels = conv_ref.shape
+    tokens, channels = conv_hbm.shape
     features = ny * LANES
     part_tokens = tokens // PARTS
     quarter = part_tokens // 2
@@ -137,6 +146,30 @@
     xr, xl, xo = lax.rem(x + 1, NX), lax.rem(x + 3, NX), lax.rem(x + 2, NX)
     yr, yl = lax.rem(y + 1, ny), lax.rem(y + ny - 1, ny)
 
+    share = pl.multiple_of((x * ny + y) * LANES, LANES)
+    taken_in = [
+        pltpu.make_async_copy(source, target, local_sem.at[k])
+        for k, (source, target) in enumerate(
+            (
+                (step_hbm, step_ref),
+                (rate_hbm, rate_ref),
+                (conv_hbm, conv_ref),
+                (b_hbm, b_ref),
+                (c_hbm, c_ref),
+                (gate_hbm, gate_ref),
+                (skip_hbm, skip_ref),
+                (ids_hbm, ids_ref),
+                (gain_hbm, gain_ref),
+                (wout_hbm, wout),
+                (resid_hbm.at[:, pl.ds(share, LANES)], resid),
+                (wexp_hbm, wexp),
+            )
+        )
+    ]
+    copy_wout, copy_resid, copy_wexp = taken_in[9:]
+    for copy in taken_in[:5]:
+        copy.start()
+
     barrier = pltpu.get_barrier_semaphore()
 
     @pl.loop(1, nz)
@@ -154,15 +187,10 @@
             barrier, inc=1, device_id={"ch": lax.rem(y + k, ny)}, device_id_type=MESH
         )
 
-    share = pl.multiple_of((x * ny + y) * LANES, LANES)
-    copy_wout = pltpu.make_async_copy(wout_hbm, wout, local_sem.at[0])
-    copy_resid = pltpu.make_async_copy(
-        resid_hbm.at[:, pl.ds(share, LANES)], resid, local_sem.at[1]
-    )
-    copy_wexp = pltpu.make_async_copy(wexp_hbm, wexp, local_sem.at[2])
-    copy_wout.start()
-    copy_resid.start()
-    copy_wexp.start()
+    for copy in taken_in[5:]:
+        copy.start()
+    for copy in taken_in[:5]:
+        copy.wait()
 
     def wide(ref):
         return jnp.concatenate(
@@ -228,6 +256,8 @@
         device = {"seq": group * STATE_GROUP + other}
         send(s1h.at[place], s1h.at[place], s1_ss.at[0], s1_rs.at[0], device)
         send(s1a.at[place], s1a.at[place], s1_ss.at[1], s1_rs.at[1], device)
+    for copy in taken_in[5:9]:
+        copy.wait()
     gates = silu(gate_ref[...].astype(F32))
     within = y_ref[...] + wide(skip_ref) * conv
     arrived(s1h.at[pl.ds(0, STATE_GROUP - 1)], s1_rs.at[0])
@@ -251,8 +281,8 @@
         @pl.when(group + k < groups)
         def _():
             device = {"seq": s + k * STATE_GROUP}
-            send(s2h.at[group], s2h.at[group], s2_ss.at[0, k], s2_rs.at[0, group], device)
-            send(s2a.at[group], s2a.at[group], s2_ss.at[1, k], s2_rs.at[1, group], device)
+            send(s2h.at[group], s2h.at[group], s2_ss.at[0], s2_rs.at[0], device)
+            send(s2a.at[group], s2a.at[group], s2_ss.at[1], s2_rs.at[1], device)
 
     names = lax.broadcasted_iota(jnp.int32, (wide_experts, tokens), 0)
     named = (ids_ref[0:1, :] == names) | (ids_ref[1:2, :] == names)
@@ -296,12 +326,17 @@
     arrange[...] = jnp.where(taken == place_of, 1.0, 0.0).astype(BF16)
 
     inc_h[...] = jnp.zeros_like(state)
+    for j in range(1, groups):
+
+        @pl.when(j == group)
+        def _():
+            arrived(s2h.at[pl.ds(0, j)], s2_rs.at[0])
+            arrived(s2a.at[pl.ds(0, j)], s2_rs.at[1])
+
     for j in range(groups - 1):
 
         @pl.when(j < group)
         def _():
-            arrived(s2h.at[j], s2_rs.at[0, j])
-            arrived(s2a.at[j], s2_rs.at[1, j])
             inc_h[...] = s2a[j] * inc_h[...] + s2h[j].astype(F32)
 
     incoming = before_a * inc_h[...] + before_h
@@ -354,22 +389,20 @@
     def pass_on(side, q, h):
         held, device = (mx_r, to_r) if side == 0 else (mx_l, to_l)
         send(
-            held.at[q, h], xn_recv.at[side, q, h], xn_ss.at[side, q, h],
-            xn_rs.at[side, q, h], device,
+            held.at[q, h], xn_recv.at[q, side, h], xn_ss.at[side], xn_rs.at[q], device,
         )
 
     def add_and_pass_on(q):
-        arrived(xo_recv.at[q, 0], xo_rs.at[q, 0])
+        arrived(xo_recv.at[q], xo_rs.at[q])
         mx_r[q, 0] = (mx_rc[q] + xo_recv[q, 0].astype(F32)).astype(BF16)
         pass_on(0, q, 0)
-        arrived(xo_recv.at[q, 1], xo_rs.at[q, 1])
         mx_l[q, 1] = (mx_lc[q] + xo_recv[q, 1].astype(F32)).astype(BF16)
         pass_on(1, q, 1)
 
     project(xo, into_opp)
     for q in range(PARTS):
-        send(mx_opp.at[q, 0], xo_recv.at[q, 0], xo_ss.at[q, 0], xo_rs.at[q, 0], to_r)
-        send(mx_opp.at[q, 1], xo_recv.at[q, 1], xo_ss.at[q, 1], xo_rs.at[q, 1], to_l)
+        send(mx_opp.at[q, 0], xo_recv.at[q, 0], xo_ss, xo_rs.at[q], to_r)
+        send(mx_opp.at[q, 1], xo_recv.at[q, 1], xo_ss, xo_rs.at[q], to_l)
     project(xr, into_r)
     pass_on(0, 0, 1)
     project(xl, into_l)
@@ -384,20 +417,18 @@
 
     far_first = sorted(range(1, ny), key=lambda k: -min(k, ny - k))
     for q in range(PARTS):
-        for side in range(2):
-            for h in (1, 0) if side == 0 else (0, 1):
-                arrived(xn_recv.at[side, q, h], xn_rs.at[side, q, h])
+        arrived(xn_recv.at[q], xn_rs.at[q])
         for n in range(ny):
             for h in range(2):
                 ysend[q, n, h * quarter : (h + 1) * quarter, :] = (
                     mx_own[q, h, n]
-                    + xn_recv[0, q, h, n].astype(F32)
-                    + xn_recv[1, q, h, n].astype(F32)
+                    + xn_recv[q, 0, h, n].astype(F32)
+                    + xn_recv[q, 1, h, n].astype(F32)
                 ).astype(BF16)
         for k in far_first:
             other = lax.rem(y + k, ny)
             send(
-                ysend.at[q, other], yrecv.at[q, y], y_ss.at[q], y_rs.at[q],
+                ysend.at[q, other], yrecv.at[q, y], y_ss, y_rs.at[q],
                 {"ch": other},
             )
         yrecv[q, y] = ysend[q, y]
@@ -460,42 +491,6 @@
             rest = jnp.concatenate([rest, jnp.zeros((16 - tail, LANES), F32)], axis=0)
         ring[y, k, main:, :] = rest.astype(BF16)
 
-    def hop_right(k, h, first_part):
-        held = lax.rem(y + ny - h + 1, ny)
-        got = lax.rem(y + ny - h, ny)
-        if first_part:
-            send(
-                ring.at[held, k], ring.at[held, k], ring_ss, ring_rs.at[0, k, h - 1],
-                {"ch": yr},
-            )
-        else:
-            arrived(ring.at[got, k], ring_rs.at[0, k, h - 1])
-
-    def hop_left(k, h, first_part):
-        held = lax.rem(y + h - 1, ny)
-        got = lax.rem(y + h, ny)
-        if first_part:
-            send(
-                ring.at[held, k], ring.at[held, k], ring_ss, ring_rs.at[1, k, h - 1],
-                {"ch": yl},
-            )
-        else:
-            arrived(ring.at[got, k], ring_rs.at[1, k, h - 1])
-
-    def hop(k, h, first_part):
-        if h < hops:
-            hop_right(k, h, first_part)
-            hop_left(k, h, first_part)
-        else:
-
-            @pl.when(even)
-            def _():
-                hop_right(k, h, first_part)
-
-            @pl.when(jnp.logical_not(even))
-            def _():
-                hop_left(k, h, first_part)
-
     gated = pb_own.shape[-1]
     width = 256
 
@@ -544,85 +539,117 @@
         arrived(s1a.at[pl.ds(0, STATE_GROUP - 1)], s1_ss.at[1])
         for k in range(1, groups):
 
-            @pl.when(group + k < groups)
+            @pl.when(group + k == groups - 1)
             def _():
-                arrived(s2h.at[0], s2_ss.at[0, k])
-                arrived(s2a.at[0], s2_ss.at[1, k])
-
-        for h in range(2):
-            for q in range(PARTS):
-                arrived(mx_opp.at[q, h], xo_ss.at[q, h])
-                arrived(mx_r.at[q, h], xn_ss.at[0, q, h])
-                arrived(mx_l.at[q, h], xn_ss.at[1, q, h])
-            arrived(pb_opp.at[h], po_ss.at[h])
-        arrived(pb_r.at[1], pn_ss.at[0, 1])
-        arrived(pb_l.at[0], pn_ss.at[1, 0])
-        for q in range(PARTS):
-            arrived(ysend.at[q, pl.ds(0, ny - 1)], y_ss.at[q])
-        for k in range(3):
-            arrived(sq_send.at[k], sq_ss.at[k])
+                arrived(s2h.at[pl.ds(0, k)], s2_ss.at[0])
+                arrived(s2a.at[pl.ds(0, k)], s2_ss.at[1])
+
+        arrived(mx_opp, xo_ss)
+        arrived(mx_r, xn_ss.at[0])
+        arrived(mx_l, xn_ss.at[1])
+        arrived(pb_opp, po_ss)
+        arrived(ysend.at[:, pl.ds(0, ny - 1)], y_ss)
+        arrived(sq_send.at[pl.ds(0, NX - 1)], sq_ss)
 
         arrived(zm_recv.at[pl.ds(0, nz - 1)], zm_ss)
         arrived(zt_recv.at[pl.ds(0, nz - 1)], zt_ss)
         arrived(ring.at[pl.ds(0, ny - 1)], ring_ss)
 
-    def exchange(k, h):
-        if h == 1:
-            fill(k)
+    def near(k):
+        return lax.rem(y + ny + k, ny)
+
+    def give(k, chunk, which, target):
+        send(
+            ring.at[chunk, k], ring.at[chunk, k], ring_ss, ring_rs.at[k, which],
+            {"ch": near(target)},
+        )
+
+    def first_round(k):
+        fill(k)
+        if hops == 4:
+            give(k, y, 0, 2)
+            give(k, y, 1, -2)
+            give(k, y, 2, 1)
+            give(k, y, 2, -1)
         else:
-            hop(k, h - 1, False)
-        if h <= hops:
-            hop(k, h, True)
-        if h == 1:
-            prepare(k, y, True)
+            for other in far_first:
+                give(k, y, 3, other)
+        prepare(k, y, True)
+
+    def second_round(k):
+        if hops == 4:
+            arrived(ring.at[near(-2), k], ring_rs.at[k, 0])
+
+            @pl.when(even)
+            def _():
+                give(k, near(-2), 3, 2)
+
+            give(k, near(-2), 3, 1)
+            arrived(ring.at[near(2), k], ring_rs.at[k, 1])
+
+            @pl.when(jnp.logical_not(even))
+            def _():
+                give(k, near(2), 3, -2)
+
+            give(k, near(2), 3, -1)
+            prepare(k, near(-2), False)
+            prepare(k, near(2), False)
+            arrived(ring.at[pl.ds(0, 2), k], ring_rs.at[k, 2])
+            prepare(k, near(-1), False)
+            prepare(k, near(1), False)
+
+    def all_in(k):
+        if hops == 4:
+            arrived(ring.at[pl.ds(0, 3), k], ring_rs.at[k, 3])
+            for other in (3, 4, 5):
+                prepare(k, near(other), False)
         else:
-            prepare(k, lax.rem(y + h - 1, ny), False)
-            if h <= hops:
-                prepare(k, lax.rem(y + ny - h + 1, ny), False)
-
-    def opposite_block():
-        exchange(0, hops + 1)
-        copy_wexp.wait()
-        for turn in range(2):
-            h = jnp.where(even, turn, 1 - turn)
-            expert_half(0, h, keep_opp)
-            device = {"exp": jnp.where(h == 0, xr, xl)}
-            send(pb_opp.at[h], po_recv.at[h], po_ss.at[h], po_rs.at[h], device)
-
-    at_turn = ((3, 6, 9, 12), (4, 7.5, 13, 16), (5, 10, 14, 17), (7, 11, 15, 18))
-    turns = sorted(
-        (at_turn[k][h - 1], k, h) for k in range(blocks) for h in range(1, hops + 1)
-    )
-    first_done = max(i for i, (_, k, _) in enumerate(turns) if k == 0)
-    for i, (_, k, h) in enumerate(turns):
-        exchange(k, h)
-        if i == min(first_done + 3, len(turns) - 1):
-            opposite_block()
-    exchange(1, hops + 1)
+            arrived(ring.at[pl.ds(0, ny - 1), k], ring_rs.at[k, 3])
+            for other in range(1, ny):
+                prepare(k, near(other), False)
+
+    def opposite_half(turn):
+        h = jnp.where(even, turn, 1 - turn)
+        expert_half(0, h, keep_opp)
+        device = {"exp": jnp.where(h == 0, xr, xl)}
+        send(pb_opp.at[h], po_recv.at[h], po_ss, po_rs.at[h], device)
+
+    first_round(0)
+    first_round(1)
+    second_round(0)
+    first_round(2)
+    second_round(1)
+    all_in(0)
+    copy_wexp.wait()
+    opposite_half(0)
+    opposite_half(1)
+    second_round(2)
+    first_round(3)
+    all_in(1)
     expert_half(1, 1, keep_r)
-    send(pb_r.at[1], pn_recv.at[0, 1], pn_ss.at[0, 1], pn_rs.at[0, 1], to_r)
-    exchange(2, hops + 1)
+    send(pb_r.at[1], pn_recv.at[0, 0], pn_ss.at[0], pn_rs.at[0], to_r)
+    all_in(2)
     expert_half(2, 0, keep_l)
-    send(pb_l.at[0], pn_recv.at[1, 0], pn_ss.at[1, 0], pn_rs.at[1, 0], to_l)
+    send(pb_l.at[0], pn_recv.at[0, 1], pn_ss.at[1], pn_rs.at[0], to_l)
+    second_round(3)
     for k, device in enumerate(({"exp": xo}, to_r, to_l)):
         square_sums(k)
-        send(sq_send.at[k], sq_recv.at[k], sq_ss.at[k], sq_rs.at[k], device)
+        send(sq_send.at[k], sq_recv.at[k], sq_ss, sq_rs, device)
     expert_half(1, 0, keep_r)
     expert_half(2, 1, keep_l)
-    exchange(3, hops + 1)
+    arrived(po_recv.at[0], po_rs.at[0])
+    pb_r[0] = (pb_rc[...] + po_recv[0].astype(F32)).astype(BF16)
+    send(pb_r.at[0], pn_recv.at[1, 0], pn_ss.at[0], pn_rs.at[1], to_r)
+    arrived(po_recv.at[1], po_rs.at[1])
+    pb_l[1] = (pb_lc[...] + po_recv[1].astype(F32)).astype(BF16)
+    send(pb_l.at[1], pn_recv.at[1, 1], pn_ss.at[1], pn_rs.at[1], to_l)
+    all_in(3)
     square_sums(3)
     for h in range(2):
         expert_half(3, h, keep_own)
-    arrived(po_recv.at[0], po_rs.at[0])
-    pb_r[0] = (pb_rc[...] + po_recv[0].astype(F32)).astype(BF16)
-    send(pb_r.at[0], pn_recv.at[0, 0], pn_ss.at[0, 0], pn_rs.at[0, 0], to_r)
-    arrived(po_recv.at[1], po_rs.at[1])
-    pb_l[1] = (pb_lc[...] + po_recv[1].astype(F32)).astype(BF16)
-    send(pb_l.at[1], pn_recv.at[1, 1], pn_ss.at[1, 1], pn_rs.at[1, 1], to_l)
 
     all_left()
-    for k in range(3):
-        arrived(sq_recv.at[k], sq_rs.at[k])
+    arrived(sq_recv, sq_rs)
     sums = sq_send[3] + sq_recv[0] + sq_recv[1] + sq_recv[2]
     inverse = lax.rsqrt(sums / (NX * features) + EPSILON)
     scale = lax.dot_general(
@@ -630,25 +657,23 @@
         precision=EXACT, preferred_element_type=F32,
     )
     scale = jnp.concatenate([scale] * (width // LANES), axis=1)
-    arrived(pn_recv.at[0, 1], pn_rs.at[0, 1])
-    pb_own[1] = pb_own[1] + pn_recv[0, 1].astype(F32)
-    arrived(pn_recv.at[1, 0], pn_rs.at[1, 0])
-    pb_own[0] = pb_own[0] + pn_recv[1, 0].astype(F32)
-    arrived(pn_recv.at[0, 0], pn_rs.at[0, 0])
-    arrived(pn_recv.at[1, 1], pn_rs.at[1, 1])
+    arrived(pn_recv.at[0], pn_rs.at[0])
+    pb_own[1] = pb_own[1] + pn_recv[0, 0].astype(F32)
+    pb_own[0] = pb_own[0] + pn_recv[0, 1].astype(F32)
+    arrived(pn_recv.at[1], pn_rs.at[1])
 
     @pl.loop(0, gated // width)
     def _(n):
         at = pl.ds(pl.multiple_of(n * width, width), width)
-        gate_part = scale * (pb_own[0, :, at] + pn_recv[0, 0, :, at].astype(F32))
+        gate_part = scale * (pb_own[0, :, at] + pn_recv[1, 0, :, at].astype(F32))
         up_part = scale * (pb_own[1, :, at] + pn_recv[1, 1, :, at].astype(F32))
         hidden = (silu(gate_part) * up_part).astype(BF16)
         out_ref[:, at] = jnp.dot(
             arrange[...], hidden, preferred_element_type=F32
         ).astype(BF16)
 
-    arrived(pb_r.at[0], pn_ss.at[0, 0])
-    arrived(pb_l.at[1], pn_ss.at[1, 1])
+    arrived(pb_r, pn_ss.at[0])
+    arrived(pb_l, pn_ss.at[1])
 
 
 def body(
@@ -683,6 +708,15 @@
     dma = pltpu.SemaphoreType.DMA
     vmem = pltpu.VMEM
     scratch = [
+        vmem((tokens, channels), BF16),
+        vmem((tokens, channels), BF16),
+        vmem((tokens, channels), BF16),
+        vmem((channels // LANES, LANES), F32),
+        vmem((entries, tokens), F32),
+        vmem((entries, tokens), F32),
+        vmem((channels // LANES, LANES), F32),
+        vmem((norm_gain.shape[0] // LANES, LANES), F32),
+        vmem((2, tokens), jnp.int32),
         vmem(out_weight.shape, BF16),
         vmem((tokens, LANES), BF16),
         vmem((features, doubled), BF16),
@@ -705,7 +739,7 @@
         vmem((PARTS, ny, quarter, LANES), F32),
         vmem((PARTS, 2, ny, quarter, LANES), F32),
         vmem((PARTS, 2, ny, quarter, LANES), BF16),
-        vmem((2, PARTS, 2, ny, quarter, LANES), BF16),
+        vmem((PARTS, 2, 2, ny, quarter, LANES), BF16),
         vmem((PARTS, ny, part_tokens, LANES), BF16),
         vmem((PARTS, ny, part_tokens, LANES), BF16),
         vmem((experts, MAIN_SLOTS, LANES), BF16),
@@ -725,29 +759,29 @@
         vmem((2, 2, rows, gated), BF16),
         vmem((NX, 8, rows), F32),
         vmem((NX - 1, 8, rows), F32),
-        dma((3,)),
+        dma((12,)),
         dma((2,)),
         dma((2,)),
-        dma((2, groups)),
-        dma((2, groups)),
-        dma((PARTS, 2)),
-        dma((PARTS, 2)),
-        dma((2, PARTS, 2)),
-        dma((2, PARTS, 2)),
+        dma((2,)),
+        dma((2,)),
+        dma,
         dma((PARTS,)),
+        dma((2,)),
+        dma((PARTS,)),
+        dma,
         dma((PARTS,)),
         dma,
         dma((NX,)),
         dma,
         dma((NX,)),
         dma,
-        dma((2, NX, hops)),
+        dma((NX, 4)),
+        dma,
         dma((2,)),
         dma((2,)),
-        dma((2, 2)),
-        dma((2, 2)),
-        dma((NX - 1,)),
-        dma((NX - 1,)),
+        dma((2,)),
+        dma,
+        dma,
     ]
     whole = pl.BlockSpec(memory_space=pltpu.VMEM)
     far = pl.BlockSpec(memory_space=pl.ANY)
@@ -755,7 +789,7 @@
     hidden = pl.pallas_call(
         functools.partial(kernel, nz, ny),
         out_shape=pltpu.VMEM((out_rows, gated), BF16),
-        in_specs=[whole] * 9 + [far] * 3,
+        in_specs=[far] * 12,
         out_specs=whole,
         scratch_shapes=scratch,
         compiler_params=pltpu.CompilerParams(collective_id=0, has_side_effects=True),

time: 92.6 us -> 87.7 us (0.947)
  Pallas kernels: 91.7 us -> 86.6 us
    pallas_call x1, Pallas kernels: 91.7 us -> 86.6 us  [body(): pl.pallas_call(functools.partial(kernel, nz, ny), out_shape=pltpu.VMEM((o...]
where the time goes in v3:
time: 87.7 us; the launch traced here: 87.3 us
  Pallas kernels  86.6 us (99%)
    pallas_call x1, Pallas kernels, body(): pl.pallas_call(functools.partial(kernel, nz, ny), out_shape=pltpu.VMEM((o...  86.6 us

profile of v3, /device:TPU:6, one launch (start us, length us, event | category | flops | bytes accessed | tf_op | source)
XLA Modules:
  0.0 87.3 jit_solution(9775131355786631005)
XLA Ops:
  0.0 86.6 %layer.1 = bf16[144,768]{1,0:T(8,128)(2,1)S(1)} custom-call(bf16[128,256]{1,0:T(8,128)(2,1)} %conv_hbm.1, bf16[128,256]{1,0:T(8,128)(2,1)} %gate_hbm.1, bf16[128,256]{1,0:T(8,128)(2,1)} %step_hbm.1, f32[2,128]{1,0:T(2,128)} %bitcast.13, f32[16,128]{1,0:T(8,128)} %bitcast.11, f32[16,128]{1,0:T(8,128)} %bitcast.12, f32[2,128]{1,0:T(2,128)} %bitcast.14, ...), custom_call_target="tpu_custom_call" | custom-call | tf_op jit(solution)/shard_map/layer/pallas_call | solution.py:789
  86.6 0.7 copy.14

commit v4 on v3

--- a/solution.py
+++ b/solution.py
@@ -172,21 +172,21 @@
 
     barrier = pltpu.get_barrier_semaphore()
 
-    @pl.loop(1, nz)
+    def greet(device):
+        pl.semaphore_signal(barrier, inc=1, device_id=device, device_id_type=MESH)
+
+    greet({"seq": lax.rem(s + nz // 2, nz)})
+
+    @pl.loop(1, nz // 2)
     def _(k):
-        pl.semaphore_signal(
-            barrier, inc=1, device_id={"seq": lax.rem(s + k, nz)}, device_id_type=MESH
-        )
+        far = nz // 2 - k
+        greet({"seq": lax.rem(s + far, nz)})
+        greet({"seq": lax.rem(s + nz - far, nz)})
 
     for k in range(1, NX):
-        pl.semaphore_signal(
-            barrier, inc=1, device_id={"exp": lax.rem(x + k, NX)}, device_id_type=MESH
-        )
+        greet({"exp": lax.rem(x + k, NX)})
     for k in range(1, ny):
-        pl.semaphore_signal(
-            barrier, inc=1, device_id={"ch": lax.rem(y + k, ny)}, device_id_type=MESH
-        )
-
+        greet({"ch": lax.rem(y + k, ny)})
     for copy in taken_in[5:]:
         copy.start()
     for copy in taken_in[:5]:
@@ -349,7 +349,7 @@
     copy_wout.wait()
 
     def project(which, store):
-        @pl.loop(0, ny // 2)
+        @pl.loop(0, ny // 2, unroll=True)
         def _(n):
             start = pl.multiple_of(which * features + n * 2 * LANES, 2 * LANES)
             part = jnp.dot(
@@ -501,7 +501,7 @@
         lhs[k, :, at] = (v * gain_ref[pl.ds(x * ny + n, 1), :]).astype(BF16)
 
     def expert_half(k, h, store):
-        @pl.loop(0, gated // width)
+        @pl.loop(0, gated // width, unroll=True)
         def _(n):
             start = pl.multiple_of(n * width, width)
             column = pl.multiple_of(h * gated + n * width, width)
@@ -564,11 +564,14 @@
             {"ch": near(target)},
         )
 
-    def first_round(k):
+    def first_round_far(k):
         fill(k)
         if hops == 4:
             give(k, y, 0, 2)
             give(k, y, 1, -2)
+
+    def first_round_near(k):
+        if hops == 4:
             give(k, y, 2, 1)
             give(k, y, 2, -1)
         else:
@@ -576,6 +579,10 @@
                 give(k, y, 3, other)
         prepare(k, y, True)
 
+    def first_round(k):
+        first_round_far(k)
+        first_round_near(k)
+
     def second_round(k):
         if hops == 4:
             arrived(ring.at[near(-2), k], ring_rs.at[k, 0])
@@ -594,6 +601,9 @@
             give(k, near(2), 3, -1)
             prepare(k, near(-2), False)
             prepare(k, near(2), False)
+
+    def neighbours_in(k):
+        if hops == 4:
             arrived(ring.at[pl.ds(0, 2), k], ring_rs.at[k, 2])
             prepare(k, near(-1), False)
             prepare(k, near(1), False)
@@ -614,9 +624,12 @@
         device = {"exp": jnp.where(h == 0, xr, xl)}
         send(pb_opp.at[h], po_recv.at[h], po_ss, po_rs.at[h], device)
 
-    first_round(0)
-    first_round(1)
+    first_round_far(0)
+    first_round_near(0)
+    first_round_far(1)
     second_round(0)
+    first_round_near(1)
+    neighbours_in(0)
     first_round(2)
     second_round(1)
     all_in(0)
@@ -625,9 +638,11 @@
     opposite_half(1)
     second_round(2)
     first_round(3)
+    neighbours_in(1)
     all_in(1)
     expert_half(1, 1, keep_r)
     send(pb_r.at[1], pn_recv.at[0, 0], pn_ss.at[0], pn_rs.at[0], to_r)
+    neighbours_in(2)
     all_in(2)
     expert_half(2, 0, keep_l)
     send(pb_l.at[0], pn_recv.at[0, 1], pn_ss.at[1], pn_rs.at[0], to_l)
@@ -643,6 +658,7 @@
     arrived(po_recv.at[1], po_rs.at[1])
     pb_l[1] = (pb_lc[...] + po_recv[1].astype(F32)).astype(BF16)
     send(pb_l.at[1], pn_recv.at[1, 1], pn_ss.at[1], pn_rs.at[1], to_l)
+    neighbours_in(3)
     all_in(3)
     square_sums(3)
     for h in range(2):
@@ -662,7 +678,7 @@
     pb_own[0] = pb_own[0] + pn_recv[0, 1].astype(F32)
     arrived(pn_recv.at[1], pn_rs.at[1])
 
-    @pl.loop(0, gated // width)
+    @pl.loop(0, gated // width, unroll=True)
     def _(n):
         at = pl.ds(pl.multiple_of(n * width, width), width)
         gate_part = scale * (pb_own[0, :, at] + pn_recv[1, 0, :, at].astype(F32))

time: 87.7 us -> 85.5 us (0.975)
  Pallas kernels: 86.6 us -> 84.6 us
    pallas_call x1, Pallas kernels: 86.6 us -> 84.6 us  [body(): pl.pallas_call(functools.partial(kernel, nz, ny), out_shape=pltpu.VMEM((o...]
where the time goes in v4:
time: 85.5 us; the launch traced here: 85.3 us
  Pallas kernels  84.6 us (99%)
    pallas_call x1, Pallas kernels, body(): pl.pallas_call(functools.partial(kernel, nz, ny), out_shape=pltpu.VMEM((o...  84.6 us

profile of v4, /device:TPU:6, one launch (start us, length us, event | category | flops | bytes accessed | tf_op | source)
XLA Modules:
  0.0 85.3 jit_solution(9545599127861470052)
XLA Ops:
  0.0 84.6 %layer.1 = bf16[144,768]{1,0:T(8,128)(2,1)S(1)} custom-call(bf16[128,256]{1,0:T(8,128)(2,1)} %conv_hbm.1, bf16[128,256]{1,0:T(8,128)(2,1)} %gate_hbm.1, bf16[128,256]{1,0:T(8,128)(2,1)} %step_hbm.1, f32[2,128]{1,0:T(2,128)} %bitcast.13, f32[16,128]{1,0:T(8,128)} %bitcast.11, f32[16,128]{1,0:T(8,128)} %bitcast.12, f32[2,128]{1,0:T(2,128)} %bitcast.14, ...), custom_call_target="tpu_custom_call" | custom-call | tf_op jit(solution)/shard_map/layer/pallas_call | solution.py:805
  84.6 0.7 copy.14

commit v5 on v4

--- a/solution.py
+++ b/solution.py
@@ -17,7 +17,7 @@
 LANES = 128
 STATE_GROUP = 4
 NX = 4
-PARTS = 4
+PARTS = 8
 
 
 def silu(v):

time: 85.5 us -> 84.6 us (0.989)
  no operation moved by 1% of the time
where the time goes in v5:
time: 84.6 us; the launch traced here: 84.5 us
  Pallas kernels  83.8 us (99%)
    pallas_call x1, Pallas kernels, body(): pl.pallas_call(functools.partial(kernel, nz, ny), out_shape=pltpu.VMEM((o...  83.8 us

profile of v5, /device:TPU:6, one launch (start us, length us, event | category | flops | bytes accessed | tf_op | source)
XLA Modules:
  0.0 84.5 jit_solution(9920579118526285645)
XLA Ops:
  0.0 83.8 %layer.1 = bf16[144,768]{1,0:T(8,128)(2,1)S(1)} custom-call(bf16[128,256]{1,0:T(8,128)(2,1)} %conv_hbm.1, bf16[128,256]{1,0:T(8,128)(2,1)} %gate_hbm.1, bf16[128,256]{1,0:T(8,128)(2,1)} %step_hbm.1, f32[2,128]{1,0:T(2,128)} %bitcast.13, f32[16,128]{1,0:T(8,128)} %bitcast.11, f32[16,128]{1,0:T(8,128)} %bitcast.12, f32[2,128]{1,0:T(2,128)} %bitcast.14, ...), custom_call_target="tpu_custom_call" | custom-call | tf_op jit(solution)/shard_map/layer/pallas_call | solution.py:805
  83.8 0.7 copy.14
